TPU v7x, 512 devices: a whole 4x8x8 slice. The times are simulated.
512 devices in a mesh: row: 128 (over y, z, core), col: 4 (over x).
Axes of the slice: x: 4, y: 8, z: 8, core: 2. Of those that a mesh axis runs over, the one named last changes fastest.
Arguments:
- tokens: bfloat16 [384, 8192], P('row', 'col'), may hold values from -6 to 6
- gate_weight: float32 [24576, 8192], P('row', 'col'), may hold values from -1 to 1
- up_weight: float32 [24576, 8192], P('row', 'col'), may hold values from -1 to 1
- down_weight: float32 [24576, 8192], P('row', 'col'), may hold values from -1 to 1
- u_init: float32 [3, 24576], P(None, 'row'), may hold values from -6 to 6
- gammas: float32 [3], replicated, may hold values from 2 to 6
Outputs:
- mixed: bfloat16 [384, 8192], P('row', 'col')
- u_out: float32 [3, 24576], P(None, 'row')
- v_out: float32 [3, 8192], P(None, 'col')
All inputs are finite; a program needn't handle non-finite values.
Results may differ from a plain program's by a relative error of at most 0.007.
Values may be sent and summed in bfloat16 or wider, within the bound.
A program may use at most 64 MiB of HBM per device.

v0:
```python
import math

import jax
import jax.numpy as jnp
from jax import lax
from jax.sharding import PartitionSpec as P

D = 8192
FF = 24576
ITERS = 2


epsilon = 1e-06
highest = lax.Precision.HIGHEST


def per_device(tokens, gate_weight, up_weight, down_weight, u_init, gammas):
    matrices = (gate_weight, up_weight, down_weight)
    lefts = [u_init[index] for index in range(3)]
    rights = lefts
    for step in range(ITERS):
        parts = [jnp.dot(lefts[index], matrices[index], precision=highest) for index in range(3)]
        backs = lax.psum((parts[0], parts[1], parts[2]), "row")
        squares = lax.psum(jnp.stack([jnp.sum(item * item) for item in backs]), "col")
        roots_back = jnp.sqrt(squares / D + epsilon)
        rights = [backs[index] / roots_back[index] for index in range(3)]
        parts = [jnp.dot(matrices[index], rights[index], precision=highest) for index in range(3)]
        fores = lax.psum((parts[0], parts[1], parts[2]), "col")
        fore_squares = lax.psum(jnp.stack([jnp.sum(item * item) for item in fores]), "row")
        roots = jnp.sqrt(fore_squares / FF + epsilon)
        lefts = [fores[index] / roots[index] for index in range(3)]
    inner = jnp.stack([jnp.sum(lefts[index] * fores[index]) for index in range(3)])
    sigmas = lax.psum(inner, "row") / math.sqrt(FF * D)
    scales = gammas / sigmas
    hidden_dev = gate_weight.shape[0]
    paired = jnp.concatenate(
        [gate_weight.astype(jnp.bfloat16), up_weight.astype(jnp.bfloat16)], axis=0
    )
    down_half = down_weight.astype(jnp.bfloat16)
    partial_sums = jnp.einsum(
        "td,fd->tf",
        lax.all_gather(tokens, "row", axis=0, tiled=True),
        paired,
        preferred_element_type=jnp.float32,
    )
    summed = lax.psum(partial_sums, "col")
    gate = summed[:, :hidden_dev] * scales[0]
    upper = summed[:, hidden_dev:] * scales[1]
    hidden = (jax.nn.silu(gate) * upper).astype(jnp.bfloat16)
    reduced = lax.psum_scatter(
        jnp.dot(hidden, down_half, preferred_element_type=jnp.float32),
        "row",
        scatter_dimension=0,
        tiled=True,
    )
    mixed = (reduced * scales[2]).astype(jnp.bfloat16)
    u_out = jnp.stack(lefts)
    v_out = jnp.stack(rights)
    return (mixed, u_out, v_out)


def solution(mesh):
    return jax.shard_map(
        per_device,
        mesh=mesh,
        in_specs=(
            P("row", "col"),
            P("row", "col"),
            P("row", "col"),
            P("row", "col"),
            P(None, "row"),
            P(),
        ),
        out_specs=(P("row", "col"), P(None, "row"), P(None, "col")),
        check_vma=False,
    )
```

profile of v0, /device:TPU:6, one launch (start us, length us, event | category | flops | bytes accessed | tf_op | source)
XLA Modules:
  0.0 2044.3 jit_solution(16368061650788715760)
XLA Ops:
  7.2 2.4 fusion.16
  9.7 0.8 fusion.18
  10.5 0.9 fusion.20
  11.4 502.2 %all-reduce.2 = (f32[2048]{0:T(1024)S(1)}, f32[2048]{0:T(1024)S(1)}, f32[2048]{0:T(1024)S(1)}) all-reduce(f32[2048]{0:T(1024)S(1)} %bitcast.104, f32[2048]{0:T(1024)S(1)} %bitcast.105, f32[2048]{0:T(1024)S(1)} %bitcast.106), channel_id=1, replica_groups=mesh['row'=128,'col'=4] {'row'}, use_global_device_ids=true, to_apply=%region_5.0 | all-reduce | flops 6144 | bytes 49152 | tf_op jit(solution)/shard_map/psum | solution.py:23
  514.8 2.0 pad_maximum_fusion.2
  516.8 7.4 psum.130
  524.9 0.6 broadcast_divide_fusion.3
  525.5 2.7 fusion.34
  528.3 0.7 broadcast_divide_fusion.4
  528.9 1.3 fusion.33
  530.3 0.7 broadcast_divide_fusion.5
  530.9 1.3 fusion.32
  532.2 10.0 all-reduce.4
  544.1 2.0 pad_maximum_fusion.3
  546.1 247.0 %psum.134 = f32[3]{0:T(128)S(1)} all-reduce(f32[3]{0:T(128)S(1)} %pad_maximum_fusion.3), channel_id=1, replica_groups=mesh['row'=128,'col'=4] {'row'}, use_global_device_ids=true, to_apply=%region_14.0 | all-reduce | flops 3 | bytes 24 | tf_op jit(solution)/shard_map/psum | solution.py:29
  793.8 0.6 broadcast_divide_fusion.9
  794.4 2.3 fusion.37
  796.7 0.6 broadcast_divide_fusion.10
  797.3 0.8 fusion.36
  798.2 0.7 broadcast_divide_fusion.11
  798.8 0.8 fusion.35
  799.7 490.9 %all-reduce.1 = (f32[2048]{0:T(1024)S(1)}, f32[2048]{0:T(1024)S(1)}, f32[2048]{0:T(1024)S(1)}) all-reduce(f32[2048]{0:T(1024)S(1)} %bitcast.101, f32[2048]{0:T(1024)S(1)} %bitcast.102, f32[2048]{0:T(1024)S(1)} %bitcast.103), channel_id=1, replica_groups=mesh['row'=128,'col'=4] {'row'}, use_global_device_ids=true, to_apply=%region_19.0 | all-reduce | flops 6144 | bytes 49152 | tf_op jit(solution)/shard_map/psum | solution.py:23
  1292.4 2.0 pad_maximum_fusion.4
  1294.4 7.7 psum.138
  1302.7 0.6 broadcast_divide_fusion
  1303.3 0.7 broadcast_divide_fusion.1
  1304.0 0.7 broadcast_divide_fusion.2
  1304.7 2.7 fusion.40
  1307.4 1.3 fusion.39
  1308.7 1.3 fusion.38
  1310.1 9.9 all-reduce.3
  1321.8 2.0 pad_maximum_fusion.5
  1323.8 246.8 %psum.142 = f32[3]{0:T(128)S(1)} all-reduce(f32[3]{0:T(128)S(1)} %pad_maximum_fusion.5), channel_id=1, replica_groups=mesh['row'=128,'col'=4] {'row'}, use_global_device_ids=true, to_apply=%region_28.0 | all-reduce | flops 3 | bytes 24 | tf_op jit(solution)/shard_map/psum | solution.py:29
  1570.6 1.0 convert_element_type.16
  1571.6 1.0 convert_element_type.15
  1573.2 1.2 multiply_reduce_fusion.6
  1574.5 1.2 multiply_reduce_fusion.7
  1575.7 3.9 reshape.7
  1579.7 3.3 fusion.4
  1583.0 1.3 multiply_reduce_fusion.8
  1584.3 1.9 pad_maximum_fusion.6
  1586.2 246.8 %psum.143 = f32[3]{0:T(128)S(1)} all-reduce(f32[3]{0:T(128)S(1)} %pad_maximum_fusion.6), channel_id=1, replica_groups=mesh['row'=128,'col'=4] {'row'}, use_global_device_ids=true, to_apply=%region_32.0 | all-reduce | flops 3 | bytes 24 | tf_op jit(solution)/shard_map/psum | solution.py:33
  1833.0 0.6 fusion.27
  1833.6 4.7 fusion.7
  1838.3 1.3 dynamic-slice
  1840.8 0.6 pad_maximum_fusion
  1841.5 194.2 %all-reduce.10.cloned.1.call-done = f32[384,2048]{1,0:T(8,128)} async-done(((f32[384,2048]{1,0:T(8,128)}), f32[384,2048]{1,0:T(8,128)}) %all-reduce.10.cloned.1.call-update) | async-done | bytes 3145744
  2035.7 2.1 fusion.15
  (39 shorter events, 9.8 us)
Async XLA Ops:
  7.2 2.5 copy-start.3
  7.2 2.5 copy-start
  7.2 3.3 copy-start.1
  7.2 1568.5 %all-gather.3.cloned.1.call-start = ((), (), s32[]{:S(2)}) async-start(), calls=%async_computation.1 | async-start | bytes 2113536 | tf_op jit(solution)/shard_map/all_gather | solution.py:42
  546.1 1287.5 %all-reduce.8.cloned.1.call-start = ((), (), s32[]{:S(2)}) async-start(), calls=%async_computation | async-start | bytes 1179648 | tf_op jit(solution)/shard_map/psum | solution.py:46
  1579.6 253.4 %copy-start.4 = (f32[3]{0:T(128)S(1)}, f32[3]{0:T(128)}, u32[]{:S(2)}) copy-start(f32[3]{0:T(128)} %param.11) | copy-start | bytes 40
  1579.7 254.0 %copy-start.2 = (f32[192,2048]{1,0:T(8,128)S(1)}, f32[192,2048]{1,0:T(8,128)}, u32[]{:S(2)}) copy-start(f32[192,2048]{1,0:T(8,128)} %param.9) | copy-start | bytes 4718596
  1583.0 452.7 %all-reduce.10.cloned.1.call-start = ((), (), s32[]{:S(2)}) async-start(), calls=%async_computation.2 | async-start | bytes 6291456
Sparse Core Ops, SparseCore 0:
  546.2 75.9 all-gather.2
  1583.1 46.0 all-reduce.7
  1838.4 197.2 all-reduce.9
where the time goes:
time: 2050 us; the launch traced here: 2040 us
  blocking collectives  1770 us (86%)
  waiting for transfers between devices  194 us (9%)
  other arithmetic  31.6 us (2%)
  matrix products  26.8 us (1%)
    psum x2, blocking collectives, per_device(): backs = lax.psum((parts[0], parts[1], parts[2]), 'row')  993 us
    psum x2, blocking collectives, per_device(): lax.psum(jnp.stack([jnp.sum(item * item) for item in fores]), 'row')  494 us
    psum x1, blocking collectives, per_device(): sigmas = lax.psum(inner, 'row') / math.sqrt(FF * D)  247 us
    unnamed x4, waiting for transfers between devices  194 us
  transfers between devices with their start and end apart: 3, of which 1 were waited for; matrix products, arithmetic and copies ran while one was open for 2% of the time, Pallas kernels for 0%

commit v1 on v0

v1 whole, which is shorter than its diff:
```python
import functools
import math

import jax
import jax.numpy as jnp
from jax import lax
from jax.experimental import pallas as pl
from jax.experimental.pallas import tpu as pltpu
from jax.sharding import PartitionSpec as P

MESH = pl.DeviceIdType.MESH
EPS = 1e-06
F32 = jnp.float32
BF16 = jnp.bfloat16


def kernel(
    dims,
    tok_h, wg_h, wu_h, wd_h, ui_h, gam,
    mixed, uout, vout,
    w, w16, d16, ui, tz, tzf, xg, xf,
    part, r1b, r1s, r2b, r2s, bv, bn,
    pk, cb, s3, r3b, s4, r4b,
    gp, xr, ga, hid, rsrc, rdst, acc, qsrc, qdst,
    wsem, lsem, p1s, p1r, p2s, p2r, p3s, p3r, cs, cr,
    e1s, e1r, e2s, e2r, ks, kr, zs, zr, ys, yr,
    gs, gr, hs, hr, fs, fr, qs, qr,
):
    NX, NY, NZ, H, D, T, DT, FT = dims
    NP = 2 * NZ
    HB = H // 8
    ZT = NZ * T
    XT = NY * ZT // NX
    row = lax.axis_index("row")
    x = lax.axis_index("col")
    y = row // NP
    q = lax.rem(row, NP)
    z = q // 2
    c = lax.rem(q, 2)

    def remote(src, dst, ssem, rsem, r, cc):
        return pltpu.make_async_remote_copy(
            src_ref=src, dst_ref=dst, send_sem=ssem, recv_sem=rsem,
            device_id={"row": r, "col": cc}, device_id_type=MESH,
        )

    def each(n, fn):
        def body(d, carry):
            fn(d)
            return carry
        lax.fori_loop(1, n, body, 0)

    def plane(d):
        p = lax.rem(q + d, NP)
        return p, y * NP + p

    def along_y(d):
        p = lax.rem(y + d, NY)
        return p, p * NP + q

    def along_z(d):
        p = lax.rem(z + d, NZ)
        return p, y * NP + p * 2 + c

    def along_x(d):
        return lax.rem(x + d, NX)

    def lanes(p, n=128):
        return pl.ds(pl.multiple_of(p * n, n), n)

    loads = [
        pltpu.make_async_copy(ui_h, ui, lsem.at[0]),
        pltpu.make_async_copy(wg_h, w.at[0], wsem.at[0]),
        pltpu.make_async_copy(wu_h, w.at[1], wsem.at[1]),
        pltpu.make_async_copy(wd_h, w.at[2], wsem.at[2]),
        pltpu.make_async_copy(tok_h, tz.at[z], lsem.at[1]),
    ]
    for load in loads:
        load.start()

    barrier = pltpu.get_barrier_semaphore()

    def greet(r, cc):
        pl.semaphore_signal(
            barrier, inc=1, device_id={"row": r, "col": cc}, device_id_type=MESH
        )

    each(NP, lambda d: greet(plane(d)[1], x))
    each(NY, lambda d: greet(along_y(d)[1], x))
    each(NX, lambda d: greet(row, along_x(d)))

    lane = lax.broadcasted_iota(jnp.int32, (8, 128), 1)
    lane1 = lax.broadcasted_iota(jnp.int32, (1, 128), 1)
    hl = lax.broadcasted_iota(jnp.int32, (8, H), 1)
    hs_ = lax.broadcasted_iota(jnp.int32, (8, H), 0)
    diag = hl - hs_

    def spread(values):
        out = jnp.zeros((1, 128), F32)
        for k in range(3):
            out = jnp.where(lane1 == k, values[k], out)
        return out

    def pick(vector, k):
        return vector[:, k : k + 1]

    def back_first():
        def body(k, carry):
            pltpu.make_async_copy(w.at[k], w.at[k], wsem.at[k]).wait()
            left = jnp.broadcast_to(ui[pl.ds(k, 1), :], (8, H))
            total = jnp.zeros((8, D), F32)
            for rb in range(HB):
                col = jnp.sum(jnp.where(diag == 8 * rb, left, 0.0), axis=1, keepdims=True)
                total = total + w[k, 8 * rb : 8 * rb + 8, :] * col
            part[0, pl.ds(k, 1), :] = jnp.sum(total, axis=0, keepdims=True)
            return carry
        lax.fori_loop(0, 3, body, 0)
        part[0, 3:4, :] = jnp.zeros((1, D), F32)

    def back_second(fore, squares):
        def body(k, carry):
            left = pltpu.roll(fore, lax.rem(128 - k * HB, 128), 1)
            total = jnp.zeros((8, D), F32)
            for rb in range(HB):
                total = total + w[k, 8 * rb : 8 * rb + 8, :] * left[:, rb : rb + 1]
            part[1, pl.ds(k, 1), :] = jnp.sum(total, axis=0, keepdims=True)
            return carry
        lax.fori_loop(0, 3, body, 0)
        line = spread(squares)
        for p in range(NP):
            part[1, 3:4, 128 * p : 128 * p + 128] = line

    def fore_packed(source):
        def body(k, packed):
            b = source[pl.ds(k, 1), :]
            b8 = jnp.broadcast_to(b, (8, D))
            mine = jnp.zeros((8, 128), F32)
            for rb in range(HB):
                got = jnp.sum(w[k, 8 * rb : 8 * rb + 8, :] * b8, axis=1, keepdims=True)
                mine = jnp.where(lane == rb, got, mine)
            packed = packed + pltpu.roll(mine, k * HB, 1)
            square = jnp.sum(b * b, axis=1, keepdims=True)
            return jnp.where(lane == 3 * HB + k, square, packed)
        return lax.fori_loop(0, 3, body, jnp.zeros((8, 128), F32))

    def leg1(t):
        return lambda d: remote(
            part.at[t, :, lanes(plane(d)[0])], r1b.at[t, q],
            p1s.at[t, d], p1r.at[t, d], plane(d)[1], x,
        )

    def leg2(t):
        return lambda d: remote(
            r1s.at[t], r2b.at[t, y], p2s.at[t, d], p2r.at[t, d], along_y(d)[1], x
        )

    def leg3(t):
        return lambda d: remote(
            r2s.at[t], bv.at[t, :, lanes(q)], p3s.at[t, d], p3r.at[t, d], plane(d)[1], x
        )

    def start1(t):
        each(NP, lambda d: leg1(t)(d).start())
        r1b[t, q] = part[t, :, lanes(q)]

    def start2(t):
        each(NP, lambda d: leg1(t)(d).wait_recv())
        total = r1b[t, 0]
        for p in range(1, NP):
            total = total + r1b[t, p]
        r1s[t] = total
        each(NY, lambda d: leg2(t)(d).start())
        r2b[t, y] = total

    def start3(t):
        each(NY, lambda d: leg2(t)(d).wait_recv())
        total = r2b[t, 0]
        for p in range(1, NY):
            total = total + r2b[t, p]
        r2s[t] = total
        each(NP, lambda d: leg3(t)(d).start())
        bv[t, :, lanes(q)] = total

    def finish3(t):
        each(NP, lambda d: leg3(t)(d).wait_recv())

    def cross(t):
        return lambda d: remote(
            pk.at[t], cb.at[t, x], cs.at[t, d], cr.at[t, d], row, along_x(d)
        )

    def col_start(t, packed):
        pk[t] = packed
        each(NX, lambda d: cross(t)(d).start())
        cb[t, x] = packed

    def col_finish(t):
        each(NX, lambda d: cross(t)(d).wait_recv())
        total = cb[t, 0]
        for p in range(1, NX):
            total = total + cb[t, p]
        roots = [
            jnp.sqrt(total[0:1, 3 * HB + k : 3 * HB + k + 1] / DT + EPS) for k in range(3)
        ]
        line = jnp.where(lane1 < HB, roots[0], jnp.where(lane1 < 2 * HB, roots[1], roots[2]))
        fore = jnp.where(lane < 3 * HB, total / line, 0.0)
        squares = []
        for k in range(3):
            own = jnp.where((lane >= k * HB) & (lane < (k + 1) * HB), fore * fore, 0.0)
            own = jnp.sum(own, axis=1, keepdims=True)
            squares.append(jnp.sum(own, axis=0, keepdims=True))
        return fore, squares, roots

    swap = [
        remote(w16.at[pl.ds(pl.multiple_of(c * H, H), H)], w16.at[pl.ds(pl.multiple_of(c * H, H), H)],
               ks.at[0], kr.at[0], row + 1 - 2 * c, x),
        remote(w16.at[pl.ds(pl.multiple_of((2 + c) * H, H), H)], w16.at[pl.ds(pl.multiple_of((2 + c) * H, H), H)],
               ks.at[1], kr.at[1], row + 1 - 2 * c, x),
        remote(d16.at[pl.ds(pl.multiple_of(c * H, H), H)], d16.at[pl.ds(pl.multiple_of(c * H, H), H)],
               ks.at[2], kr.at[2], row + 1 - 2 * c, x),
    ]

    def tokens_z(d):
        return remote(tok_h, tz.at[z], zs.at[d], zr.at[d], along_z(d)[1], x)

    def tokens_y(d):
        return remote(xg.at[y], xg.at[y], ys.at[d], yr.at[d], along_y(d)[1], x)

    def gates_out(d):
        return remote(
            gp.at[pl.ds(pl.multiple_of(along_x(d) * XT, XT), XT)], xr.at[x],
            gs.at[d], gr.at[d], row, along_x(d),
        )

    def gates_back(d):
        mine = ga.at[pl.ds(pl.multiple_of(x * XT, XT), XT)]
        return remote(mine, mine, hs.at[d], hr.at[d], row, along_x(d))

    def sums_y(d):
        return remote(rsrc.at[along_y(d)[0]], rdst.at[y], fs.at[d], fr.at[d], along_y(d)[1], x)

    def sums_z(d):
        return remote(qsrc.at[along_z(d)[0]], qdst.at[z], qs.at[d], qr.at[d], along_z(d)[1], x)

    loads[0].wait()
    back_first()
    pl.semaphore_wait(barrier, (NP - 1) + (NY - 1) + (NX - 1))
    start1(0)
    each(NZ, lambda d: tokens_z(d).start())
    w16[pl.ds(pl.multiple_of(c * H, H), H), :] = w[0].astype(BF16)
    swap[0].start()
    w16[pl.ds(pl.multiple_of((2 + c) * H, H), H), :] = w[1].astype(BF16)
    swap[1].start()
    start2(0)

    loads[4].wait()
    each(NZ, lambda d: tokens_z(d).wait_recv())
    for p in range(NZ):
        tzf[T * p : T * p + T, :] = tz[p].astype(F32)
    xg[y] = tzf[...].astype(BF16)
    each(NY, lambda d: tokens_y(d).start())
    start3(0)

    d16[pl.ds(pl.multiple_of(c * H, H), H), :] = w[2].astype(BF16)
    swap[2].start()
    finish3(0)
    col_start(0, fore_packed(bv.at[0]))
    fore, squares, _ = col_finish(0)
    back_second(fore, squares)
    start1(1)

    each(NY, lambda d: tokens_y(d).wait_recv())
    for p in range(NY):
        xf[ZT * p : ZT * p + ZT, :] = xg[p].astype(F32)
    swap[0].wait_recv()
    swap[1].wait_recv()

    width = min(256, 4 * H)

    def gate_block(n, carry):
        gp[:, lanes(n, width)] = lax.dot_general(
            xf[...].astype(BF16), w16[pl.ds(pl.multiple_of(n * width, width), width), :],
            (((1,), (1,)), ((), ())), preferred_element_type=F32,
        )
        return carry

    lax.fori_loop(0, 4 * H // width, gate_block, 0)
    each(NX, lambda d: gates_out(d).start())
    xr[x] = gp[pl.ds(pl.multiple_of(x * XT, XT), XT), :]

    start2(1)
    start3(1)
    each(NX, lambda d: gates_out(d).wait_recv())
    total = xr[0]
    for p in range(1, NX):
        total = total + xr[p]
    ga[pl.ds(pl.multiple_of(x * XT, XT), XT), :] = total
    each(NX, lambda d: gates_back(d).start())
    finish3(1)

    line = bv[1, 3:4, 0:128]
    for k in range(3):
        bn[k : k + 1, :] = bv[1, k : k + 1, :] / jnp.sqrt(pick(line, k) / FT + EPS)
    col_start(1, fore_packed(bn))
    fore, squares, roots = col_finish(1)

    def len1(d):
        return remote(s3, r3b.at[q], e1s.at[d], e1r.at[d], plane(d)[1], x)

    def len2(d):
        return remote(s4, r4b.at[y], e2s.at[d], e2r.at[d], along_y(d)[1], x)

    line = spread(squares)
    s3[...] = line
    each(NP, lambda d: len1(d).start())
    r3b[q] = line
    for k in range(3):
        vout[k : k + 1, :] = bn[k : k + 1, :] / roots[k]
    each(NX, lambda d: gates_back(d).wait_recv())
    each(NP, lambda d: len1(d).wait_recv())
    line = r3b[0]
    for p in range(1, NP):
        line = line + r3b[p]
    s4[...] = line
    each(NY, lambda d: len2(d).start())
    r4b[y] = line
    swap[2].wait_recv()
    each(NY, lambda d: len2(d).wait_recv())
    line = r4b[0]
    for p in range(1, NY):
        line = line + r4b[p]

    lengths = [jnp.sqrt(pick(line, k) / FT + EPS) for k in range(3)]
    sigmas = [pick(line, k) / lengths[k] / math.sqrt(FT * DT) for k in range(3)]
    scales = [gam[k] / sigmas[k] for k in range(3)]

    gate = ga[:, 0 : 2 * H] * scales[0]
    upper = ga[:, 2 * H : 4 * H] * scales[1]
    hid[...] = (gate * jax.nn.sigmoid(gate) * upper).astype(BF16)

    def down_block(n, carry):
        out = jnp.dot(hid[...], d16[:, lanes(n, 256)], preferred_element_type=F32)
        for p in range(NY):
            rsrc[p, :, lanes(n, 256)] = out[ZT * p : ZT * p + ZT].astype(BF16)
        return carry

    lax.fori_loop(0, D // 256, down_block, 0)
    each(NY, lambda d: sums_y(d).start())
    rdst[y] = rsrc[y]

    left = fore / jnp.where(lane1 < HB, lengths[0], jnp.where(lane1 < 2 * HB, lengths[1], lengths[2]))

    def unpack(k, carry):
        own = pltpu.roll(left, lax.rem(128 - k * HB, 128), 1)
        rows = jnp.zeros((8, H), F32)
        for rb in range(HB):
            rows = jnp.where(diag == 8 * rb, own[:, rb : rb + 1], rows)
        keep = (diag >= 0) & (lax.rem(diag, 8) == 0)
        rows = jnp.where(keep, rows, 0.0)
        uout[pl.ds(k, 1), :] = jnp.sum(rows, axis=0, keepdims=True)
        return carry

    lax.fori_loop(0, 3, unpack, 0)

    each(NY, lambda d: sums_y(d).wait_recv())
    total = rdst[0].astype(F32)
    for p in range(1, NY):
        total = total + rdst[p].astype(F32)
    acc[...] = total
    for p in range(NZ):
        qsrc[p] = acc[T * p : T * p + T, :].astype(BF16)
    each(NZ, lambda d: sums_z(d).start())
    qdst[z] = qsrc[z]
    each(NZ, lambda d: sums_z(d).wait_recv())
    total = qdst[0].astype(F32)
    for p in range(1, NZ):
        total = total + qdst[p].astype(F32)
    mixed[...] = (total * scales[2]).astype(BF16)

    for t in range(2):
        each(NP, lambda d: leg1(t)(d).wait_send())
        each(NY, lambda d: leg2(t)(d).wait_send())
        each(NP, lambda d: leg3(t)(d).wait_send())
        each(NX, lambda d: cross(t)(d).wait_send())
    for copy in swap:
        copy.wait_send()
    each(NZ, lambda d: tokens_z(d).wait_send())
    each(NY, lambda d: tokens_y(d).wait_send())
    each(NX, lambda d: gates_out(d).wait_send())
    each(NX, lambda d: gates_back(d).wait_send())
    each(NP, lambda d: len1(d).wait_send())
    each(NY, lambda d: len2(d).wait_send())
    each(NY, lambda d: sums_y(d).wait_send())
    each(NZ, lambda d: sums_z(d).wait_send())


def solution(mesh):
    rows, NX = mesh.shape["row"], mesh.shape["col"]
    NZ = math.isqrt(rows // 2)
    NY = rows // 2 // NZ
    NP = 2 * NZ

    def per_device(tokens, gate_weight, up_weight, down_weight, u_init, gammas):
        T, D = tokens.shape
        H = gate_weight.shape[0]
        ZT = NZ * T
        NT = NY * ZT
        XT = NT // NX
        dims = (NX, NY, NZ, H, D, T, D * NX, H * rows)
        V = pltpu.VMEM
        dma = pltpu.SemaphoreType.DMA
        anywhere = pl.BlockSpec(memory_space=pl.ANY)
        vmem = pl.BlockSpec(memory_space=pltpu.VMEM)
        return pl.pallas_call(
            functools.partial(kernel, dims),
            out_shape=(
                jax.ShapeDtypeStruct((T, D), BF16),
                jax.ShapeDtypeStruct((3, H), F32),
                jax.ShapeDtypeStruct((3, D), F32),
            ),
            in_specs=[anywhere] * 5 + [pl.BlockSpec(memory_space=pltpu.SMEM)],
            out_specs=(vmem, vmem, vmem),
            scratch_shapes=[
                V((3, H, D), F32), V((4 * H, D), BF16), V((2 * H, D), BF16), V((3, H), F32),
                V((NZ, T, D), BF16), V((ZT, D), F32), V((NY, ZT, D), BF16), V((NT, D), F32),
                V((2, 4, D), F32), V((2, NP, 4, 128), F32), V((2, 4, 128), F32),
                V((2, NY, 4, 128), F32), V((2, 4, 128), F32), V((2, 4, D), F32), V((3, D), F32),
                V((2, 8, 128), F32), V((2, NX, 8, 128), F32),
                V((1, 128), F32), V((NP, 1, 128), F32), V((1, 128), F32), V((NY, 1, 128), F32),
                V((NT, 4 * H), F32), V((NX, XT, 4 * H), F32), V((NT, 4 * H), F32), V((NT, 2 * H), BF16),
                V((NY, ZT, D), BF16), V((NY, ZT, D), BF16), V((ZT, D), F32),
                V((NZ, T, D), BF16), V((NZ, T, D), BF16),
                dma((3,)), dma((2,)),
                dma((2, NP)), dma((2, NP)), dma((2, NY)), dma((2, NY)), dma((2, NP)), dma((2, NP)),
                dma((2, NX)), dma((2, NX)),
                dma((NP,)), dma((NP,)), dma((NY,)), dma((NY,)), dma((3,)), dma((3,)),
                dma((NZ,)), dma((NZ,)), dma((NY,)), dma((NY,)),
                dma((NX,)), dma((NX,)), dma((NX,)), dma((NX,)),
                dma((NY,)), dma((NY,)), dma((NZ,)), dma((NZ,)),
            ],
            compiler_params=pltpu.CompilerParams(
                collective_id=0, has_side_effects=True, vmem_limit_bytes=60 * 1024 * 1024
            ),
        )(tokens, gate_weight, up_weight, down_weight, u_init, gammas)

    return jax.shard_map(
        per_device,
        mesh=mesh,
        in_specs=(
            P("row", "col"),
            P("row", "col"),
            P("row", "col"),
            P("row", "col"),
            P(None, "row"),
            P(),
        ),
        out_specs=(P("row", "col"), P(None, "row"), P(None, "col")),
        check_vma=False,
    )
```

time: 2050 us -> 104 us (0.05)
  the two profiles are of different devices: /device:TPU:6 before, /device:TPU:16 now
where the time goes in v1:
time: 104 us; the launch traced here: 103 us
  Pallas kernels  98.8 us (95%)
  local copies, waits for them, and re-layouts  3.97 us (4%)
    pallas_call x1, Pallas kernels, per_device(): pl.pallas_call(functools.partial(kernel, dims), out_shape=(jax.ShapeDtype...  98.8 us
    unnamed x3, local copies, waits for them, and re-layouts  3.97 us

profile of v1, /device:TPU:16, one launch (start us, length us, event | category | flops | bytes accessed | tf_op | source)
XLA Modules:
  0.0 103.4 jit_solution(5676932349905536498)
XLA Ops:
  0.6 98.8 %shard_map.85 = (bf16[3,2048]{1,0:T(4,128)(2,1)}, f32[3,192]{1,0:T(4,128)}, f32[3,2048]{1,0:T(4,128)}) custom-call(bf16[3,2048]{1,0:T(4,128)(2,1)} %tok_h.1, f32[192,2048]{1,0:T(8,128)} %wg_h.1, f32[192,2048]{1,0:T(8,128)} %wu_h.1, f32[192,2048]{1,0:T(8,128)} %wd_h.1, f32[3,192]{1,0:T(4,128)} %ui_h.1, f32[3]{0:T(128)} %gam.1), custom_call_target="tpu_custom_call" | custom-call | tf_op jit(solution)/shard_map/pallas_call | solution.py:414
  99.4 1.3 %copy.12 = bf16[3,2048]{1,0:T(4,128)(2,1)} copy(bf16[3,2048]{1,0:T(4,128)(2,1)} %get-tuple-element.6) | data formatting | bytes 24576
  100.8 1.3 %copy.13 = f32[3,192]{1,0:T(4,128)} copy(f32[3,192]{1,0:T(4,128)} %get-tuple-element.7) | data formatting | bytes 4608
  102.0 1.4 %copy.14 = f32[3,2048]{1,0:T(4,128)} copy(f32[3,2048]{1,0:T(4,128)} %get-tuple-element.8) | data formatting | bytes 49152

commit v2 on v1

--- a/solution.py
+++ b/solution.py
@@ -16,21 +16,23 @@
 
 def kernel(
     dims,
-    tok_h, wg_h, wu_h, wd_h, ui_h, gam,
+    tok_h, wg_h, wu_h, wd_h, ui_h, gam_h,
     mixed, uout, vout,
-    w, w16, d16, ui, tz, tzf, xg, xf,
+    gam, w, w16, d16, ui, ta, tb, tzf, xa, xb, xf, x16, perm,
     part, r1b, r1s, r2b, r2s, bv, bn,
     pk, cb, s3, r3b, s4, r4b,
-    gp, xr, ga, hid, rsrc, rdst, acc, qsrc, qdst,
+    gp, xr, ga, hid, asrc, adst, bsrc, bdst, acc, aq, ar, bq, br,
     wsem, lsem, p1s, p1r, p2s, p2r, p3s, p3r, cs, cr,
-    e1s, e1r, e2s, e2r, ks, kr, zs, zr, ys, yr,
-    gs, gr, hs, hr, fs, fr, qs, qr,
+    e1s, e1r, e2s, e2r, ks, kr, ta1s, ta1r, tb1s, tb1r, ta2s, ta2r, tb2s, tb2r,
+    gs, gr, hs, hr, as1, ar1, bs1, br1, as2, ar2, bs2, br2,
 ):
     NX, NY, NZ, H, D, T, DT, FT = dims
     NP = 2 * NZ
     HB = H // 8
     ZT = NZ * T
+    YT = NY * T
     XT = NY * ZT // NX
+    W = D // 2
     row = lax.axis_index("row")
     x = lax.axis_index("col")
     y = row // NP
@@ -73,7 +75,9 @@
         pltpu.make_async_copy(wg_h, w.at[0], wsem.at[0]),
         pltpu.make_async_copy(wu_h, w.at[1], wsem.at[1]),
         pltpu.make_async_copy(wd_h, w.at[2], wsem.at[2]),
-        pltpu.make_async_copy(tok_h, tz.at[z], lsem.at[1]),
+        pltpu.make_async_copy(tok_h.at[:, 0:W], ta.at[z], lsem.at[1]),
+        pltpu.make_async_copy(tok_h.at[:, W:D], tb.at[y], lsem.at[2]),
+        pltpu.make_async_copy(gam_h, gam, lsem.at[3]),
     ]
     for load in loads:
         load.start()
@@ -220,11 +224,17 @@
                ks.at[2], kr.at[2], row + 1 - 2 * c, x),
     ]
 
-    def tokens_z(d):
-        return remote(tok_h, tz.at[z], zs.at[d], zr.at[d], along_z(d)[1], x)
-
-    def tokens_y(d):
-        return remote(xg.at[y], xg.at[y], ys.at[d], yr.at[d], along_y(d)[1], x)
+    def tok_a1(d):
+        return remote(tok_h.at[:, 0:W], ta.at[z], ta1s.at[d], ta1r.at[d], along_z(d)[1], x)
+
+    def tok_b1(d):
+        return remote(tok_h.at[:, W:D], tb.at[y], tb1s.at[d], tb1r.at[d], along_y(d)[1], x)
+
+    def tok_a2(d):
+        return remote(xa.at[y], xa.at[y], ta2s.at[d], ta2r.at[d], along_y(d)[1], x)
+
+    def tok_b2(d):
+        return remote(xb.at[z], xb.at[z], tb2s.at[d], tb2r.at[d], along_z(d)[1], x)
 
     def gates_out(d):
         return remote(
@@ -236,55 +246,76 @@
         mine = ga.at[pl.ds(pl.multiple_of(x * XT, XT), XT)]
         return remote(mine, mine, hs.at[d], hr.at[d], row, along_x(d))
 
-    def sums_y(d):
-        return remote(rsrc.at[along_y(d)[0]], rdst.at[y], fs.at[d], fr.at[d], along_y(d)[1], x)
-
-    def sums_z(d):
-        return remote(qsrc.at[along_z(d)[0]], qdst.at[z], qs.at[d], qr.at[d], along_z(d)[1], x)
+    def sum_a1(d):
+        return remote(asrc.at[along_y(d)[0]], adst.at[y], as1.at[d], ar1.at[d], along_y(d)[1], x)
+
+    def sum_b1(d):
+        return remote(bsrc.at[along_z(d)[0]], bdst.at[z], bs1.at[d], br1.at[d], along_z(d)[1], x)
+
+    def sum_a2(d):
+        return remote(aq.at[along_z(d)[0]], ar.at[z], as2.at[d], ar2.at[d], along_z(d)[1], x)
+
+    def sum_b2(d):
+        return remote(bq.at[along_y(d)[0]], br.at[y], bs2.at[d], br2.at[d], along_y(d)[1], x)
 
     loads[0].wait()
     back_first()
     pl.semaphore_wait(barrier, (NP - 1) + (NY - 1) + (NX - 1))
     start1(0)
-    each(NZ, lambda d: tokens_z(d).start())
+    each(NZ, lambda d: tok_a1(d).start())
+    each(NY, lambda d: tok_b1(d).start())
     w16[pl.ds(pl.multiple_of(c * H, H), H), :] = w[0].astype(BF16)
     swap[0].start()
     w16[pl.ds(pl.multiple_of((2 + c) * H, H), H), :] = w[1].astype(BF16)
     swap[1].start()
-    start2(0)
-
-    loads[4].wait()
-    each(NZ, lambda d: tokens_z(d).wait_recv())
-    for p in range(NZ):
-        tzf[T * p : T * p + T, :] = tz[p].astype(F32)
-    xg[y] = tzf[...].astype(BF16)
-    each(NY, lambda d: tokens_y(d).start())
-    start3(0)
-
     d16[pl.ds(pl.multiple_of(c * H, H), H), :] = w[2].astype(BF16)
     swap[2].start()
+    start2(0)
+
+    loads[4].wait()
+    each(NZ, lambda d: tok_a1(d).wait_recv())
+    for p in range(NZ):
+        tzf[T * p : T * p + T, :] = ta[p].astype(F32)
+    xa[y] = tzf[...].astype(BF16)
+    each(NY, lambda d: tok_a2(d).start())
+    loads[5].wait()
+    each(NY, lambda d: tok_b1(d).wait_recv())
+    for p in range(NY):
+        tzf[T * p : T * p + T, :] = tb[p].astype(F32)
+    xb[z] = tzf[...].astype(BF16)
+    lo = lax.broadcasted_iota(jnp.int32, (NY * ZT, NY * ZT), 0)
+    hi = lax.broadcasted_iota(jnp.int32, (NY * ZT, NY * ZT), 1)
+    major = jnp.zeros_like(lo)
+    for p in range(1, NY):
+        major = major + (lo >= p * ZT).astype(jnp.int32)
+    minor = jnp.zeros_like(lo)
+    for p in range(1, NZ):
+        minor = minor + (lo - major * ZT >= p * T).astype(jnp.int32)
+    wanted = minor * YT + major * T + (lo - major * ZT - minor * T)
+    perm[...] = jnp.where(hi == wanted, 1.0, 0.0).astype(BF16)
+    start3(0)
+    each(NZ, lambda d: tok_b2(d).start())
     finish3(0)
     col_start(0, fore_packed(bv.at[0]))
     fore, squares, _ = col_finish(0)
     back_second(fore, squares)
     start1(1)
 
-    each(NY, lambda d: tokens_y(d).wait_recv())
+    each(NY, lambda d: tok_a2(d).wait_recv())
     for p in range(NY):
-        xf[ZT * p : ZT * p + ZT, :] = xg[p].astype(F32)
+        xf[ZT * p : ZT * p + ZT, :] = xa[p].astype(F32)
+    x16[:, 0:W] = xf[...].astype(BF16)
+    each(NZ, lambda d: tok_b2(d).wait_recv())
+    for p in range(NZ):
+        xf[YT * p : YT * p + YT, :] = xb[p].astype(F32)
+    x16[:, W:D] = jnp.dot(
+        perm[...], xf[...].astype(BF16), preferred_element_type=F32
+    ).astype(BF16)
     swap[0].wait_recv()
     swap[1].wait_recv()
-
-    width = min(256, 4 * H)
-
-    def gate_block(n, carry):
-        gp[:, lanes(n, width)] = lax.dot_general(
-            xf[...].astype(BF16), w16[pl.ds(pl.multiple_of(n * width, width), width), :],
-            (((1,), (1,)), ((), ())), preferred_element_type=F32,
-        )
-        return carry
-
-    lax.fori_loop(0, 4 * H // width, gate_block, 0)
+    gp[...] = lax.dot_general(
+        x16[...], w16[...], (((1,), (1,)), ((), ())), preferred_element_type=F32
+    )
     each(NX, lambda d: gates_out(d).start())
     xr[x] = gp[pl.ds(pl.multiple_of(x * XT, XT), XT), :]
 
@@ -295,13 +326,13 @@
     for p in range(1, NX):
         total = total + xr[p]
     ga[pl.ds(pl.multiple_of(x * XT, XT), XT), :] = total
-    each(NX, lambda d: gates_back(d).start())
     finish3(1)
 
     line = bv[1, 3:4, 0:128]
     for k in range(3):
         bn[k : k + 1, :] = bv[1, k : k + 1, :] / jnp.sqrt(pick(line, k) / FT + EPS)
     col_start(1, fore_packed(bn))
+    each(NX, lambda d: gates_back(d).start())
     fore, squares, roots = col_finish(1)
 
     def len1(d):
@@ -316,7 +347,6 @@
     r3b[q] = line
     for k in range(3):
         vout[k : k + 1, :] = bn[k : k + 1, :] / roots[k]
-    each(NX, lambda d: gates_back(d).wait_recv())
     each(NP, lambda d: len1(d).wait_recv())
     line = r3b[0]
     for p in range(1, NP):
@@ -325,11 +355,13 @@
     each(NY, lambda d: len2(d).start())
     r4b[y] = line
     swap[2].wait_recv()
+    each(NX, lambda d: gates_back(d).wait_recv())
     each(NY, lambda d: len2(d).wait_recv())
     line = r4b[0]
     for p in range(1, NY):
         line = line + r4b[p]
 
+    loads[6].wait()
     lengths = [jnp.sqrt(pick(line, k) / FT + EPS) for k in range(3)]
     sigmas = [pick(line, k) / lengths[k] / math.sqrt(FT * DT) for k in range(3)]
     scales = [gam[k] / sigmas[k] for k in range(3)]
@@ -338,15 +370,17 @@
     upper = ga[:, 2 * H : 4 * H] * scales[1]
     hid[...] = (gate * jax.nn.sigmoid(gate) * upper).astype(BF16)
 
-    def down_block(n, carry):
-        out = jnp.dot(hid[...], d16[:, lanes(n, 256)], preferred_element_type=F32)
-        for p in range(NY):
-            rsrc[p, :, lanes(n, 256)] = out[ZT * p : ZT * p + ZT].astype(BF16)
-        return carry
-
-    lax.fori_loop(0, D // 256, down_block, 0)
-    each(NY, lambda d: sums_y(d).start())
-    rdst[y] = rsrc[y]
+    out = jnp.dot(hid[...], d16[:, 0:W], preferred_element_type=F32)
+    for p in range(NY):
+        asrc[p] = out[ZT * p : ZT * p + ZT].astype(BF16)
+    each(NY, lambda d: sum_a1(d).start())
+    turned = jnp.dot(perm[...], hid[...], preferred_element_type=F32).astype(BF16)
+    out = jnp.dot(turned, d16[:, W:D], preferred_element_type=F32)
+    for p in range(NZ):
+        bsrc[p] = out[YT * p : YT * p + YT].astype(BF16)
+    each(NZ, lambda d: sum_b1(d).start())
+    adst[y] = asrc[y]
+    bdst[z] = bsrc[z]
 
     left = fore / jnp.where(lane1 < HB, lengths[0], jnp.where(lane1 < 2 * HB, lengths[1], lengths[2]))
 
@@ -362,21 +396,6 @@
 
     lax.fori_loop(0, 3, unpack, 0)
 
-    each(NY, lambda d: sums_y(d).wait_recv())
-    total = rdst[0].astype(F32)
-    for p in range(1, NY):
-        total = total + rdst[p].astype(F32)
-    acc[...] = total
-    for p in range(NZ):
-        qsrc[p] = acc[T * p : T * p + T, :].astype(BF16)
-    each(NZ, lambda d: sums_z(d).start())
-    qdst[z] = qsrc[z]
-    each(NZ, lambda d: sums_z(d).wait_recv())
-    total = qdst[0].astype(F32)
-    for p in range(1, NZ):
-        total = total + qdst[p].astype(F32)
-    mixed[...] = (total * scales[2]).astype(BF16)
-
     for t in range(2):
         each(NP, lambda d: leg1(t)(d).wait_send())
         each(NY, lambda d: leg2(t)(d).wait_send())
@@ -384,14 +403,47 @@
         each(NX, lambda d: cross(t)(d).wait_send())
     for copy in swap:
         copy.wait_send()
-    each(NZ, lambda d: tokens_z(d).wait_send())
-    each(NY, lambda d: tokens_y(d).wait_send())
+    each(NZ, lambda d: tok_a1(d).wait_send())
+    each(NY, lambda d: tok_b1(d).wait_send())
+    each(NY, lambda d: tok_a2(d).wait_send())
+    each(NZ, lambda d: tok_b2(d).wait_send())
     each(NX, lambda d: gates_out(d).wait_send())
     each(NX, lambda d: gates_back(d).wait_send())
     each(NP, lambda d: len1(d).wait_send())
     each(NY, lambda d: len2(d).wait_send())
-    each(NY, lambda d: sums_y(d).wait_send())
-    each(NZ, lambda d: sums_z(d).wait_send())
+
+    each(NY, lambda d: sum_a1(d).wait_recv())
+    total = adst[0].astype(F32)
+    for p in range(1, NY):
+        total = total + adst[p].astype(F32)
+    acc[...] = total
+    for p in range(NZ):
+        aq[p] = acc[T * p : T * p + T, :].astype(BF16)
+    each(NZ, lambda d: sum_a2(d).start())
+    ar[z] = aq[z]
+    each(NZ, lambda d: sum_b1(d).wait_recv())
+    total = bdst[0].astype(F32)
+    for p in range(1, NZ):
+        total = total + bdst[p].astype(F32)
+    acc[...] = total
+    for p in range(NY):
+        bq[p] = acc[T * p : T * p + T, :].astype(BF16)
+    each(NY, lambda d: sum_b2(d).start())
+    br[y] = bq[y]
+    each(NY, lambda d: sum_a1(d).wait_send())
+    each(NZ, lambda d: sum_b1(d).wait_send())
+    each(NZ, lambda d: sum_a2(d).wait_recv())
+    total = ar[0].astype(F32)
+    for p in range(1, NZ):
+        total = total + ar[p].astype(F32)
+    mixed[:, 0:W] = (total * scales[2]).astype(BF16)
+    each(NY, lambda d: sum_b2(d).wait_recv())
+    total = br[0].astype(F32)
+    for p in range(1, NY):
+        total = total + br[p].astype(F32)
+    mixed[:, W:D] = (total * scales[2]).astype(BF16)
+    each(NZ, lambda d: sum_a2(d).wait_send())
+    each(NY, lambda d: sum_b2(d).wait_send())
 
 
 def solution(mesh):
@@ -406,6 +458,8 @@
         ZT = NZ * T
         NT = NY * ZT
         XT = NT // NX
+        W = D // 2
+        YT = NY * T
         dims = (NX, NY, NZ, H, D, T, D * NX, H * rows)
         V = pltpu.VMEM
         dma = pltpu.SemaphoreType.DMA
@@ -414,29 +468,31 @@
         return pl.pallas_call(
             functools.partial(kernel, dims),
             out_shape=(
-                jax.ShapeDtypeStruct((T, D), BF16),
-                jax.ShapeDtypeStruct((3, H), F32),
-                jax.ShapeDtypeStruct((3, D), F32),
+                V((T, D), BF16),
+                V((3, H), F32),
+                V((3, D), F32),
             ),
-            in_specs=[anywhere] * 5 + [pl.BlockSpec(memory_space=pltpu.SMEM)],
+            in_specs=[anywhere] * 6,
             out_specs=(vmem, vmem, vmem),
             scratch_shapes=[
+                pltpu.SMEM((3,), F32),
                 V((3, H, D), F32), V((4 * H, D), BF16), V((2 * H, D), BF16), V((3, H), F32),
-                V((NZ, T, D), BF16), V((ZT, D), F32), V((NY, ZT, D), BF16), V((NT, D), F32),
+                V((NZ, T, W), BF16), V((NY, T, W), BF16), V((ZT, W), F32),
+                V((NY, ZT, W), BF16), V((NZ, YT, W), BF16), V((NT, W), F32), V((NT, D), BF16), V((NT, NT), BF16),
                 V((2, 4, D), F32), V((2, NP, 4, 128), F32), V((2, 4, 128), F32),
                 V((2, NY, 4, 128), F32), V((2, 4, 128), F32), V((2, 4, D), F32), V((3, D), F32),
                 V((2, 8, 128), F32), V((2, NX, 8, 128), F32),
                 V((1, 128), F32), V((NP, 1, 128), F32), V((1, 128), F32), V((NY, 1, 128), F32),
                 V((NT, 4 * H), F32), V((NX, XT, 4 * H), F32), V((NT, 4 * H), F32), V((NT, 2 * H), BF16),
-                V((NY, ZT, D), BF16), V((NY, ZT, D), BF16), V((ZT, D), F32),
-                V((NZ, T, D), BF16), V((NZ, T, D), BF16),
-                dma((3,)), dma((2,)),
+                V((NY, ZT, W), BF16), V((NY, ZT, W), BF16), V((NZ, YT, W), BF16), V((NZ, YT, W), BF16), V((ZT, W), F32),
+                V((NZ, T, W), BF16), V((NZ, T, W), BF16), V((NY, T, W), BF16), V((NY, T, W), BF16),
+                dma((3,)), dma((4,)),
                 dma((2, NP)), dma((2, NP)), dma((2, NY)), dma((2, NY)), dma((2, NP)), dma((2, NP)),
                 dma((2, NX)), dma((2, NX)),
                 dma((NP,)), dma((NP,)), dma((NY,)), dma((NY,)), dma((3,)), dma((3,)),
-                dma((NZ,)), dma((NZ,)), dma((NY,)), dma((NY,)),
+                dma((NZ,)), dma((NZ,)), dma((NY,)), dma((NY,)), dma((NY,)), dma((NY,)), dma((NZ,)), dma((NZ,)),
                 dma((NX,)), dma((NX,)), dma((NX,)), dma((NX,)),
-                dma((NY,)), dma((NY,)), dma((NZ,)), dma((NZ,)),
+                dma((NY,)), dma((NY,)), dma((NZ,)), dma((NZ,)), dma((NZ,)), dma((NZ,)), dma((NY,)), dma((NY,)),
             ],
             compiler_params=pltpu.CompilerParams(
                 collective_id=0, has_side_effects=True, vmem_limit_bytes=60 * 1024 * 1024

time: 104 us -> 86.6 us (0.83)
  the two profiles are of different devices: /device:TPU:16 before, /device:TPU:6 now
where the time goes in v2:
time: 86.6 us; the launch traced here: 86.5 us
  Pallas kernels  84 us (97%)
  local copies, waits for them, and re-layouts  1.81 us (2%)
    pallas_call x1, Pallas kernels, per_device(): pl.pallas_call(functools.partial(kernel, dims), out_shape=(V((T, D), BF16...  84 us
    unnamed x3, local copies, waits for them, and re-layouts  1.81 us

profile of v2, /device:TPU:6, one launch (start us, length us, event | category | flops | bytes accessed | tf_op | source)
XLA Modules:
  0.0 86.5 jit_solution(14781752804220255520)
XLA Ops:
  0.6 84.0 %shard_map.85 = (bf16[3,2048]{1,0:T(4,128)(2,1)S(1)}, f32[3,192]{1,0:T(4,128)S(1)}, f32[3,2048]{1,0:T(4,128)S(1)}) custom-call(bf16[3,2048]{1,0:T(4,128)(2,1)} %tok_h.1, f32[192,2048]{1,0:T(8,128)} %wg_h.1, f32[192,2048]{1,0:T(8,128)} %wu_h.1, f32[192,2048]{1,0:T(8,128)} %wd_h.1, f32[3,192]{1,0:T(4,128)} %ui_h.1, f32[3]{0:T(128)} %gam_h.1), custom_call_target="tpu_custom_call" | custom-call | tf_op jit(solution)/shard_map/pallas_call | solution.py:468
  84.7 0.6 copy.12
  85.3 0.6 copy.13
  85.9 0.6 copy.14

commit v3 on v2

v3 whole, which is shorter than its diff:
```python
import functools
import math

import jax
import jax.numpy as jnp
from jax import lax
from jax.experimental import pallas as pl
from jax.experimental.pallas import tpu as pltpu
from jax.sharding import PartitionSpec as P

MESH = pl.DeviceIdType.MESH
EPS = 1e-06
F32 = jnp.float32
BF16 = jnp.bfloat16


def kernel(
    dims,
    tok_h, wg_h, wu_h, wd_h, ui_h, gam_h,
    mixed, uout, vout,
    gam, w, w16, d16, ui, ta, tb, tzf, xa, xb, xf, x16, perm,
    part_0, r1b_0, r1s_0, r2b_0, r2s_0, bv_0, bn_0, pk_0, cb_0, s3_0, r3b_0, s4_0, r4b_0,
    part_1, r1b_1, r1s_1, r2b_1, r2s_1, bv_1, bn_1, pk_1, cb_1, s3_1, r3b_1, s4_1, r4b_1,
    gp, xr, ga, hid, asrc, adst, bsrc, bdst, acc, aq, ar, bq, br,
    wsem, lsem, p1s, p1r, p2s, p2r, p3s, p3r, cs, cr,
    e1s, e1r, e2s, e2r, ks, kr, ta1s, ta1r, tb1s, tb1r, ta2s, ta2r, tb2s, tb2r,
    gs, gr, hs, hr, as1, ar1, bs1, br1, as2, ar2, bs2, br2,
):
    NX, NY, NZ, H, D, T, DT, FT = dims
    FIRST, N, ROWS = (0, 1), (1, 2), (2, 4)
    part, r1b, r1s, r2b, r2s = (part_0, part_1), (r1b_0, r1b_1), (r1s_0, r1s_1), (r2b_0, r2b_1), (r2s_0, r2s_1)
    bv, bn, pk, cb = (bv_0, bv_1), (bn_0, bn_1), (pk_0, pk_1), (cb_0, cb_1)
    s3, r3b, s4, r4b = (s3_0, s3_1), (r3b_0, r3b_1), (s4_0, s4_1), (r4b_0, r4b_1)
    NP = 2 * NZ
    HB = H // 8
    ZT = NZ * T
    YT = NY * T
    XT = NY * ZT // NX
    W = D // 2
    row = lax.axis_index("row")
    x = lax.axis_index("col")
    y = row // NP
    q = lax.rem(row, NP)
    z = q // 2
    c = lax.rem(q, 2)

    def remote(src, dst, ssem, rsem, r, cc):
        return pltpu.make_async_remote_copy(
            src_ref=src, dst_ref=dst, send_sem=ssem, recv_sem=rsem,
            device_id={"row": r, "col": cc}, device_id_type=MESH,
        )

    def each(n, fn):
        def body(d, carry):
            fn(d)
            return carry
        lax.fori_loop(1, n, body, 0)

    def plane(d):
        p = lax.rem(q + d, NP)
        return p, y * NP + p

    def along_y(d):
        p = lax.rem(y + d, NY)
        return p, p * NP + q

    def along_z(d):
        p = lax.rem(z + d, NZ)
        return p, y * NP + p * 2 + c

    def along_x(d):
        return lax.rem(x + d, NX)

    def lanes(p, n=128):
        return pl.ds(pl.multiple_of(p * n, n), n)

    barrier = pltpu.get_barrier_semaphore()

    def greet(r, cc):
        pl.semaphore_signal(
            barrier, inc=1, device_id={"row": r, "col": cc}, device_id_type=MESH
        )

    each(NP, lambda d: greet(plane(d)[1], x))
    each(NY, lambda d: greet(along_y(d)[1], x))
    each(NX, lambda d: greet(row, along_x(d)))

    loads = [
        pltpu.make_async_copy(ui_h, ui, lsem.at[0]),
        pltpu.make_async_copy(wg_h, w.at[0], wsem.at[0]),
        pltpu.make_async_copy(wu_h, w.at[1], wsem.at[1]),
        pltpu.make_async_copy(wd_h, w.at[2], wsem.at[2]),
        pltpu.make_async_copy(tok_h.at[:, 0:W], ta.at[z], lsem.at[1]),
        pltpu.make_async_copy(tok_h.at[:, W:D], tb.at[y], lsem.at[2]),
        pltpu.make_async_copy(gam_h, gam, lsem.at[3]),
    ]
    for load in loads:
        load.start()

    lane = lax.broadcasted_iota(jnp.int32, (8, 128), 1)
    lane1 = lax.broadcasted_iota(jnp.int32, (1, 128), 1)
    hl = lax.broadcasted_iota(jnp.int32, (8, H), 1)
    hs_ = lax.broadcasted_iota(jnp.int32, (8, H), 0)
    diag = hl - hs_

    def spread(values):
        out = jnp.zeros((1, 128), F32)
        for k, value in enumerate(values):
            out = jnp.where(lane1 == k, value, out)
        return out

    def per_block(values):
        out = values[-1]
        for k in reversed(range(len(values) - 1)):
            out = jnp.where(lane1 < (k + 1) * HB, values[k], out)
        return out

    def pick(vector, k):
        return vector[:, k : k + 1]

    def back_first(g):
        def body(j, carry):
            k = FIRST[g] + j
            pltpu.make_async_copy(w.at[k], w.at[k], wsem.at[k]).wait()
            left = jnp.broadcast_to(ui[pl.ds(k, 1), :], (8, H))
            total = jnp.zeros((8, D), F32)
            for rb in range(HB):
                col = jnp.sum(jnp.where(diag == 8 * rb, left, 0.0), axis=1, keepdims=True)
                total = total + w[k, 8 * rb : 8 * rb + 8, :] * col
            part[g][0, pl.ds(j, 1), :] = jnp.sum(total, axis=0, keepdims=True)
            return carry
        lax.fori_loop(0, N[g], body, 0)
        part[g][0, N[g] : ROWS[g], :] = jnp.zeros((ROWS[g] - N[g], D), F32)

    def back_second(g, fore, squares):
        def body(j, carry):
            left = pltpu.roll(fore, lax.rem(128 - j * HB, 128), 1)
            total = jnp.zeros((8, D), F32)
            for rb in range(HB):
                total = total + w[FIRST[g] + j, 8 * rb : 8 * rb + 8, :] * left[:, rb : rb + 1]
            part[g][1, pl.ds(j, 1), :] = jnp.sum(total, axis=0, keepdims=True)
            return carry
        lax.fori_loop(0, N[g], body, 0)
        line = jnp.broadcast_to(spread(squares), (ROWS[g] - N[g], 128))
        for p in range(NP):
            part[g][1, N[g] : ROWS[g], 128 * p : 128 * p + 128] = line

    def fore_packed(g, source):
        def body(j, packed):
            b = source[pl.ds(j, 1), :]
            b8 = jnp.broadcast_to(b, (8, D))
            mine = jnp.zeros((8, 128), F32)
            for rb in range(HB):
                got = jnp.sum(w[FIRST[g] + j, 8 * rb : 8 * rb + 8, :] * b8, axis=1, keepdims=True)
                mine = jnp.where(lane == rb, got, mine)
            packed = packed + pltpu.roll(mine, j * HB, 1)
            square = jnp.sum(b * b, axis=1, keepdims=True)
            return jnp.where(lane == N[g] * HB + j, square, packed)
        return lax.fori_loop(0, N[g], body, jnp.zeros((8, 128), F32))

    def leg1(g, t):
        return lambda d: remote(
            part[g].at[t, :, lanes(plane(d)[0])], r1b[g].at[t, q],
            p1s.at[g, t, d], p1r.at[g, t, d], plane(d)[1], x,
        )

    def leg2(g, t):
        return lambda d: remote(
            r1s[g].at[t], r2b[g].at[t, y], p2s.at[g, t, d], p2r.at[g, t, d], along_y(d)[1], x
        )

    def leg3(g, t):
        return lambda d: remote(
            r2s[g].at[t], bv[g].at[t, :, lanes(q)], p3s.at[g, t, d], p3r.at[g, t, d], plane(d)[1], x
        )

    def start1(g, t):
        each(NP, lambda d: leg1(g, t)(d).start())
        r1b[g][t, q] = part[g][t, :, lanes(q)]

    def start2(g, t):
        each(NP, lambda d: leg1(g, t)(d).wait_recv())
        total = r1b[g][t, 0]
        for p in range(1, NP):
            total = total + r1b[g][t, p]
        r1s[g][t] = total
        each(NY, lambda d: leg2(g, t)(d).start())
        r2b[g][t, y] = total

    def start3(g, t):
        each(NY, lambda d: leg2(g, t)(d).wait_recv())
        total = r2b[g][t, 0]
        for p in range(1, NY):
            total = total + r2b[g][t, p]
        r2s[g][t] = total
        each(NP, lambda d: leg3(g, t)(d).start())
        bv[g][t, :, lanes(q)] = total

    def finish3(g, t):
        each(NP, lambda d: leg3(g, t)(d).wait_recv())

    def normalise(g):
        line = bv[g][1, N[g] : N[g] + 1, 0:128]
        for j in range(N[g]):
            bn[g][j : j + 1, :] = bv[g][1, j : j + 1, :] / jnp.sqrt(pick(line, j) / FT + EPS)

    def cross(g, t):
        return lambda d: remote(
            pk[g].at[t], cb[g].at[t, x], cs.at[g, t, d], cr.at[g, t, d], row, along_x(d)
        )

    def col_start(g, t, packed):
        pk[g][t] = packed
        each(NX, lambda d: cross(g, t)(d).start())
        cb[g][t, x] = packed

    def col_finish(g, t):
        each(NX, lambda d: cross(g, t)(d).wait_recv())
        total = cb[g][t, 0]
        for p in range(1, NX):
            total = total + cb[g][t, p]
        base = N[g] * HB
        roots = [
            jnp.sqrt(total[0:1, base + j : base + j + 1] / DT + EPS) for j in range(N[g])
        ]
        fore = jnp.where(lane < base, total / per_block(roots), 0.0)
        squares = []
        for j in range(N[g]):
            own = jnp.where((lane >= j * HB) & (lane < (j + 1) * HB), fore * fore, 0.0)
            own = jnp.sum(own, axis=1, keepdims=True)
            squares.append(jnp.sum(own, axis=0, keepdims=True))
        return fore, squares, roots

    def len1(g):
        return lambda d: remote(
            s3[g], r3b[g].at[q], e1s.at[g, d], e1r.at[g, d], plane(d)[1], x
        )

    def len2(g):
        return lambda d: remote(
            s4[g], r4b[g].at[y], e2s.at[g, d], e2r.at[g, d], along_y(d)[1], x
        )

    def lengths_start(g, squares):
        line = spread(squares)
        s3[g][...] = line
        each(NP, lambda d: len1(g)(d).start())
        r3b[g][q] = line

    def lengths_turn(g):
        each(NP, lambda d: len1(g)(d).wait_recv())
        line = r3b[g][0]
        for p in range(1, NP):
            line = line + r3b[g][p]
        s4[g][...] = line
        each(NY, lambda d: len2(g)(d).start())
        r4b[g][y] = line

    def lengths_finish(g):
        each(NY, lambda d: len2(g)(d).wait_recv())
        line = r4b[g][0]
        for p in range(1, NY):
            line = line + r4b[g][p]
        lengths = [jnp.sqrt(pick(line, j) / FT + EPS) for j in range(N[g])]
        sigmas = [pick(line, j) / lengths[j] / math.sqrt(FT * DT) for j in range(N[g])]
        return lengths, [gam[FIRST[g] + j] / sigmas[j] for j in range(N[g])]

    def left_out(g, fore, lengths):
        left = fore / per_block(lengths)
        keep = (diag >= 0) & (lax.rem(diag, 8) == 0)

        def unpack(j, carry):
            own = pltpu.roll(left, lax.rem(128 - j * HB, 128), 1)
            rows = jnp.zeros((8, H), F32)
            for rb in range(HB):
                rows = jnp.where(diag == 8 * rb, own[:, rb : rb + 1], rows)
            rows = jnp.where(keep, rows, 0.0)
            uout[pl.ds(FIRST[g] + j, 1), :] = jnp.sum(rows, axis=0, keepdims=True)
            return carry

        lax.fori_loop(0, N[g], unpack, 0)

    def right_out(g, roots):
        for j in range(N[g]):
            vout[FIRST[g] + j : FIRST[g] + j + 1, :] = bn[g][j : j + 1, :] / roots[j]

    swap = [
        remote(w16.at[pl.ds(pl.multiple_of(c * H, H), H)], w16.at[pl.ds(pl.multiple_of(c * H, H), H)],
               ks.at[0], kr.at[0], row + 1 - 2 * c, x),
        remote(w16.at[pl.ds(pl.multiple_of((2 + c) * H, H), H)], w16.at[pl.ds(pl.multiple_of((2 + c) * H, H), H)],
               ks.at[1], kr.at[1], row + 1 - 2 * c, x),
        remote(d16.at[pl.ds(pl.multiple_of(c * H, H), H)], d16.at[pl.ds(pl.multiple_of(c * H, H), H)],
               ks.at[2], kr.at[2], row + 1 - 2 * c, x),
    ]

    def tok_a1(d):
        return remote(tok_h.at[:, 0:W], ta.at[z], ta1s.at[d], ta1r.at[d], along_z(d)[1], x)

    def tok_b1(d):
        return remote(tok_h.at[:, W:D], tb.at[y], tb1s.at[d], tb1r.at[d], along_y(d)[1], x)

    def tok_a2(d):
        return remote(xa.at[y], xa.at[y], ta2s.at[d], ta2r.at[d], along_y(d)[1], x)

    def tok_b2(d):
        return remote(xb.at[z], xb.at[z], tb2s.at[d], tb2r.at[d], along_z(d)[1], x)

    def gates_out(d):
        return remote(
            gp.at[pl.ds(pl.multiple_of(along_x(d) * XT, XT), XT)], xr.at[x],
            gs.at[d], gr.at[d], row, along_x(d),
        )

    def gates_back(d):
        mine = ga.at[pl.ds(pl.multiple_of(x * XT, XT), XT)]
        return remote(mine, mine, hs.at[d], hr.at[d], row, along_x(d))

    def sum_a1(d):
        return remote(asrc.at[along_y(d)[0]], adst.at[y], as1.at[d], ar1.at[d], along_y(d)[1], x)

    def sum_b1(d):
        return remote(bsrc.at[along_z(d)[0]], bdst.at[z], bs1.at[d], br1.at[d], along_z(d)[1], x)

    def sum_a2(d):
        return remote(aq.at[along_z(d)[0]], ar.at[z], as2.at[d], ar2.at[d], along_z(d)[1], x)

    def sum_b2(d):
        return remote(bq.at[along_y(d)[0]], br.at[y], bs2.at[d], br2.at[d], along_y(d)[1], x)

    loads[0].wait()
    back_first(0)
    back_first(1)
    pl.semaphore_wait(barrier, (NP - 1) + (NY - 1) + (NX - 1))
    start1(0, 0)
    start1(1, 0)
    each(NZ, lambda d: tok_a1(d).start())
    each(NY, lambda d: tok_b1(d).start())
    w16[pl.ds(pl.multiple_of(c * H, H), H), :] = w[0].astype(BF16)
    w16[pl.ds(pl.multiple_of((2 + c) * H, H), H), :] = w[1].astype(BF16)
    d16[pl.ds(pl.multiple_of(c * H, H), H), :] = w[2].astype(BF16)
    start2(0, 0)
    start2(1, 0)

    loads[4].wait()
    each(NZ, lambda d: tok_a1(d).wait_recv())
    for p in range(NZ):
        tzf[T * p : T * p + T, :] = ta[p].astype(F32)
    xa[y] = tzf[...].astype(BF16)
    each(NY, lambda d: tok_a2(d).start())
    loads[5].wait()
    each(NY, lambda d: tok_b1(d).wait_recv())
    for p in range(NY):
        tzf[T * p : T * p + T, :] = tb[p].astype(F32)
    xb[z] = tzf[...].astype(BF16)
    lo = lax.broadcasted_iota(jnp.int32, (NY * ZT, NY * ZT), 0)
    hi = lax.broadcasted_iota(jnp.int32, (NY * ZT, NY * ZT), 1)
    major = jnp.zeros_like(lo)
    for p in range(1, NY):
        major = major + (lo >= p * ZT).astype(jnp.int32)
    minor = jnp.zeros_like(lo)
    for p in range(1, NZ):
        minor = minor + (lo - major * ZT >= p * T).astype(jnp.int32)
    wanted = minor * YT + major * T + (lo - major * ZT - minor * T)
    perm[...] = jnp.where(hi == wanted, 1.0, 0.0).astype(BF16)
    start3(0, 0)
    start3(1, 0)
    each(NZ, lambda d: tok_b2(d).start())
    finish3(0, 0)
    col_start(0, 0, fore_packed(0, bv[0].at[0]))
    finish3(1, 0)
    col_start(1, 0, fore_packed(1, bv[1].at[0]))
    for copy in swap:
        copy.start()
    fore, squares, _ = col_finish(0, 0)
    back_second(0, fore, squares)
    start1(0, 1)
    fore, squares, _ = col_finish(1, 0)
    back_second(1, fore, squares)
    start1(1, 1)

    each(NY, lambda d: tok_a2(d).wait_recv())
    for p in range(NY):
        xf[ZT * p : ZT * p + ZT, :] = xa[p].astype(F32)
    x16[:, 0:W] = xf[...].astype(BF16)
    each(NZ, lambda d: tok_b2(d).wait_recv())
    for p in range(NZ):
        xf[YT * p : YT * p + YT, :] = xb[p].astype(F32)
    x16[:, W:D] = jnp.dot(
        perm[...], xf[...].astype(BF16), preferred_element_type=F32
    ).astype(BF16)
    swap[0].wait_recv()
    swap[1].wait_recv()
    gp[...] = lax.dot_general(
        x16[...], w16[...], (((1,), (1,)), ((), ())), preferred_element_type=F32
    )
    each(NX, lambda d: gates_out(d).start())
    xr[x] = gp[pl.ds(pl.multiple_of(x * XT, XT), XT), :]

    start2(0, 1)
    start2(1, 1)
    start3(0, 1)
    start3(1, 1)
    each(NX, lambda d: gates_out(d).wait_recv())
    total = xr[0]
    for p in range(1, NX):
        total = total + xr[p]
    ga[pl.ds(pl.multiple_of(x * XT, XT), XT), :] = total
    finish3(0, 1)
    normalise(0)
    col_start(0, 1, fore_packed(0, bn[0]))
    finish3(1, 1)
    normalise(1)
    col_start(1, 1, fore_packed(1, bn[1]))
    each(NX, lambda d: gates_back(d).start())
    fore_0, squares, roots_0 = col_finish(0, 1)
    lengths_start(0, squares)
    fore_1, squares, roots_1 = col_finish(1, 1)
    lengths_start(1, squares)
    right_out(0, roots_0)
    right_out(1, roots_1)
    lengths_turn(0)
    lengths_turn(1)
    swap[2].wait_recv()
    each(NX, lambda d: gates_back(d).wait_recv())
    loads[6].wait()
    lengths_0, scales_0 = lengths_finish(0)
    gate = ga[:, 0 : 2 * H] * scales_0[0]
    upper = ga[:, 2 * H : 4 * H]
    hid[...] = (gate * jax.nn.sigmoid(gate) * upper).astype(BF16)

    out = jnp.dot(hid[...], d16[:, 0:W], preferred_element_type=F32)
    for p in range(NY):
        asrc[p] = out[ZT * p : ZT * p + ZT].astype(BF16)
    each(NY, lambda d: sum_a1(d).start())
    turned = jnp.dot(perm[...], hid[...], preferred_element_type=F32).astype(BF16)
    out = jnp.dot(turned, d16[:, W:D], preferred_element_type=F32)
    for p in range(NZ):
        bsrc[p] = out[YT * p : YT * p + YT].astype(BF16)
    each(NZ, lambda d: sum_b1(d).start())
    adst[y] = asrc[y]
    bdst[z] = bsrc[z]

    lengths_1, scales_1 = lengths_finish(1)
    left_out(0, fore_0, lengths_0)
    left_out(1, fore_1, lengths_1)

    for g in range(2):
        for t in range(2):
            each(NP, lambda d: leg1(g, t)(d).wait_send())
            each(NY, lambda d: leg2(g, t)(d).wait_send())
            each(NP, lambda d: leg3(g, t)(d).wait_send())
            each(NX, lambda d: cross(g, t)(d).wait_send())
        each(NP, lambda d: len1(g)(d).wait_send())
        each(NY, lambda d: len2(g)(d).wait_send())
    for copy in swap:
        copy.wait_send()
    each(NZ, lambda d: tok_a1(d).wait_send())
    each(NY, lambda d: tok_b1(d).wait_send())
    each(NY, lambda d: tok_a2(d).wait_send())
    each(NZ, lambda d: tok_b2(d).wait_send())
    each(NX, lambda d: gates_out(d).wait_send())
    each(NX, lambda d: gates_back(d).wait_send())

    each(NY, lambda d: sum_a1(d).wait_recv())
    total = adst[0].astype(F32)
    for p in range(1, NY):
        total = total + adst[p].astype(F32)
    acc[...] = total
    for p in range(NZ):
        aq[p] = acc[T * p : T * p + T, :].astype(BF16)
    each(NZ, lambda d: sum_a2(d).start())
    ar[z] = aq[z]
    each(NZ, lambda d: sum_b1(d).wait_recv())
    total = bdst[0].astype(F32)
    for p in range(1, NZ):
        total = total + bdst[p].astype(F32)
    acc[...] = total
    for p in range(NY):
        bq[p] = acc[T * p : T * p + T, :].astype(BF16)
    each(NY, lambda d: sum_b2(d).start())
    br[y] = bq[y]
    each(NY, lambda d: sum_a1(d).wait_send())
    each(NZ, lambda d: sum_b1(d).wait_send())
    each(NZ, lambda d: sum_a2(d).wait_recv())
    total = ar[0].astype(F32)
    for p in range(1, NZ):
        total = total + ar[p].astype(F32)
    mixed[:, 0:W] = (total * scales_1[0] * scales_1[1]).astype(BF16)
    each(NY, lambda d: sum_b2(d).wait_recv())
    total = br[0].astype(F32)
    for p in range(1, NY):
        total = total + br[p].astype(F32)
    mixed[:, W:D] = (total * scales_1[0] * scales_1[1]).astype(BF16)
    each(NZ, lambda d: sum_a2(d).wait_send())
    each(NY, lambda d: sum_b2(d).wait_send())


def hand_over(a, b, c, d, e, f, sems):
    copies = [
        pltpu.make_async_copy(source, target, sems.at[i])
        for i, (source, target) in enumerate(((a, d), (b, e), (c, f)))
    ]
    for copy in copies:
        copy.start()
    for copy in copies:
        copy.wait()


def solution(mesh):
    rows, NX = mesh.shape["row"], mesh.shape["col"]
    NZ = math.isqrt(rows // 2)
    NY = rows // 2 // NZ
    NP = 2 * NZ

    def per_device(tokens, gate_weight, up_weight, down_weight, u_init, gammas):
        T, D = tokens.shape
        H = gate_weight.shape[0]
        ZT = NZ * T
        NT = NY * ZT
        XT = NT // NX
        W = D // 2
        YT = NY * T
        dims = (NX, NY, NZ, H, D, T, D * NX, H * rows)
        V = pltpu.VMEM
        dma = pltpu.SemaphoreType.DMA

        def group(rows, n):
            return [
                V((2, rows, D), F32), V((2, NP, rows, 128), F32), V((2, rows, 128), F32),
                V((2, NY, rows, 128), F32), V((2, rows, 128), F32), V((2, rows, D), F32), V((n, D), F32),
                V((2, 8, 128), F32), V((2, NX, 8, 128), F32),
                V((1, 128), F32), V((NP, 1, 128), F32), V((1, 128), F32), V((NY, 1, 128), F32),
            ]

        anywhere = pl.BlockSpec(memory_space=pl.ANY)
        vmem = pl.BlockSpec(memory_space=pltpu.VMEM)
        held = pl.pallas_call(
            functools.partial(kernel, dims),
            out_shape=(
                V((T, D), BF16),
                V((3, H), F32),
                V((3, D), F32),
            ),
            in_specs=[anywhere] * 6,
            out_specs=(vmem, vmem, vmem),
            scratch_shapes=[
                pltpu.SMEM((3,), F32),
                V((3, H, D), F32), V((4 * H, D), BF16), V((2 * H, D), BF16), V((3, H), F32),
                V((NZ, T, W), BF16), V((NY, T, W), BF16), V((ZT, W), F32),
                V((NY, ZT, W), BF16), V((NZ, YT, W), BF16), V((NT, W), F32), V((NT, D), BF16), V((NT, NT), BF16),
                *(ref for g in range(2) for ref in group((2, 4)[g], (1, 2)[g])),
                V((NT, 4 * H), F32), V((NX, XT, 4 * H), F32), V((NT, 4 * H), F32), V((NT, 2 * H), BF16),
                V((NY, ZT, W), BF16), V((NY, ZT, W), BF16), V((NZ, YT, W), BF16), V((NZ, YT, W), BF16), V((ZT, W), F32),
                V((NZ, T, W), BF16), V((NZ, T, W), BF16), V((NY, T, W), BF16), V((NY, T, W), BF16),
                dma((3,)), dma((4,)),
                dma((2, 2, NP)), dma((2, 2, NP)), dma((2, 2, NY)), dma((2, 2, NY)), dma((2, 2, NP)), dma((2, 2, NP)),
                dma((2, 2, NX)), dma((2, 2, NX)),
                dma((2, NP)), dma((2, NP)), dma((2, NY)), dma((2, NY)), dma((3,)), dma((3,)),
                dma((NZ,)), dma((NZ,)), dma((NY,)), dma((NY,)), dma((NY,)), dma((NY,)), dma((NZ,)), dma((NZ,)),
                dma((NX,)), dma((NX,)), dma((NX,)), dma((NX,)),
                dma((NY,)), dma((NY,)), dma((NZ,)), dma((NZ,)), dma((NZ,)), dma((NZ,)), dma((NY,)), dma((NY,)),
            ],
            compiler_params=pltpu.CompilerParams(
                collective_id=0, has_side_effects=True, vmem_limit_bytes=60 * 1024 * 1024
            ),
        )(tokens, gate_weight, up_weight, down_weight, u_init, gammas)
        return pl.pallas_call(
            hand_over,
            out_shape=tuple(jax.ShapeDtypeStruct(v.shape, v.dtype) for v in held),
            in_specs=[vmem] * 3,
            out_specs=(anywhere,) * 3,
            scratch_shapes=[dma((3,))],
            compiler_params=pltpu.CompilerParams(vmem_limit_bytes=1024 * 1024),
        )(*held)

    return jax.shard_map(
        per_device,
        mesh=mesh,
        in_specs=(
            P("row", "col"),
            P("row", "col"),
            P("row", "col"),
            P("row", "col"),
            P(None, "row"),
            P(),
        ),
        out_specs=(P("row", "col"), P(None, "row"), P(None, "col")),
        check_vma=False,
    )
```

time: 86.6 us -> 84.7 us (0.978)
  local copies, waits for them, and re-layouts: 1.81 us -> 0 us
    unnamed x3 -> x0, local copies, waits for them, and re-layouts: 1.81 us -> none
where the time goes in v3:
time: 84.7 us; the launch traced here: 84.6 us
  Pallas kernels  83.9 us (99%)
    pallas_call x1, Pallas kernels, per_device(): pl.pallas_call(functools.partial(kernel, dims), out_shape=(V((T, D), BF16...  83.3 us

profile of v3, /device:TPU:6, one launch (start us, length us, event | category | flops | bytes accessed | tf_op | source)
XLA Modules:
  0.0 84.6 jit_solution(13505715079035391674)
XLA Ops:
  0.6 83.3 %shard_map.85 = (bf16[3,2048]{1,0:T(4,128)(2,1)S(1)}, f32[3,192]{1,0:T(4,128)S(1)}, f32[3,2048]{1,0:T(4,128)S(1)}) custom-call(bf16[3,2048]{1,0:T(4,128)(2,1)} %tok_h.1, f32[192,2048]{1,0:T(8,128)} %wg_h.1, f32[192,2048]{1,0:T(8,128)} %wu_h.1, f32[192,2048]{1,0:T(8,128)} %wd_h.1, f32[3,192]{1,0:T(4,128)} %ui_h.1, f32[3]{0:T(128)} %gam_h.1), custom_call_target="tpu_custom_call" | custom-call | tf_op jit(solution)/shard_map/pallas_call | solution.py:537
  83.9 0.7 shard_map.86

commit v4 on v3

--- a/solution.py
+++ b/solution.py
@@ -21,7 +21,7 @@
     gam, w, w16, d16, ui, ta, tb, tzf, xa, xb, xf, x16, perm,
     part_0, r1b_0, r1s_0, r2b_0, r2s_0, bv_0, bn_0, pk_0, cb_0, s3_0, r3b_0, s4_0, r4b_0,
     part_1, r1b_1, r1s_1, r2b_1, r2s_1, bv_1, bn_1, pk_1, cb_1, s3_1, r3b_1, s4_1, r4b_1,
-    gp, xr, ga, hid, asrc, adst, bsrc, bdst, acc, aq, ar, bq, br,
+    gp, xr, ga, hid, asrc, adst, bsrc, bdst, acc, acb, aq, ar, bq, br,
     wsem, lsem, p1s, p1r, p2s, p2r, p3s, p3r, cs, cr,
     e1s, e1r, e2s, e2r, ks, kr, ta1s, ta1r, tb1s, tb1r, ta2s, ta2r, tb2s, tb2r,
     gs, gr, hs, hr, as1, ar1, bs1, br1, as2, ar2, bs2, br2,
@@ -37,12 +37,13 @@
     YT = NY * T
     XT = NY * ZT // NX
     W = D // 2
+    Q = W // 2
     row = lax.axis_index("row")
     x = lax.axis_index("col")
     y = row // NP
-    q = lax.rem(row, NP)
+    q = row & (NP - 1)
     z = q // 2
-    c = lax.rem(q, 2)
+    c = q & 1
 
     def remote(src, dst, ssem, rsem, r, cc):
         return pltpu.make_async_remote_copy(
@@ -51,25 +52,26 @@
         )
 
     def each(n, fn):
-        def body(d, carry):
+        for d in sorted(range(1, n), key=lambda d: -min(d, n - d)):
             fn(d)
-            return carry
-        lax.fori_loop(1, n, body, 0)
+
+    def turn(at, d, n):
+        return (at + d) & (n - 1)
 
     def plane(d):
-        p = lax.rem(q + d, NP)
+        p = turn(q, d, NP)
         return p, y * NP + p
 
     def along_y(d):
-        p = lax.rem(y + d, NY)
+        p = turn(y, d, NY)
         return p, p * NP + q
 
     def along_z(d):
-        p = lax.rem(z + d, NZ)
+        p = turn(z, d, NZ)
         return p, y * NP + p * 2 + c
 
     def along_x(d):
-        return lax.rem(x + d, NX)
+        return turn(x, d, NX)
 
     def lanes(p, n=128):
         return pl.ds(pl.multiple_of(p * n, n), n)
@@ -81,8 +83,8 @@
             barrier, inc=1, device_id={"row": r, "col": cc}, device_id_type=MESH
         )
 
+    each(NY, lambda d: greet(along_y(d)[1], x))
     each(NP, lambda d: greet(plane(d)[1], x))
-    each(NY, lambda d: greet(along_y(d)[1], x))
     each(NX, lambda d: greet(row, along_x(d)))
 
     loads = [
@@ -315,11 +317,11 @@
         mine = ga.at[pl.ds(pl.multiple_of(x * XT, XT), XT)]
         return remote(mine, mine, hs.at[d], hr.at[d], row, along_x(d))
 
-    def sum_a1(d):
-        return remote(asrc.at[along_y(d)[0]], adst.at[y], as1.at[d], ar1.at[d], along_y(d)[1], x)
-
-    def sum_b1(d):
-        return remote(bsrc.at[along_z(d)[0]], bdst.at[z], bs1.at[d], br1.at[d], along_z(d)[1], x)
+    def sum_a1(d, h):
+        return remote(asrc.at[along_y(d)[0], h], adst.at[y, h], as1.at[h, d], ar1.at[h, d], along_y(d)[1], x)
+
+    def sum_b1(d, h):
+        return remote(bsrc.at[along_z(d)[0], h], bdst.at[z, h], bs1.at[h, d], br1.at[h, d], along_z(d)[1], x)
 
     def sum_a2(d):
         return remote(aq.at[along_z(d)[0]], ar.at[z], as2.at[d], ar2.at[d], along_z(d)[1], x)
@@ -419,7 +421,6 @@
     right_out(0, roots_0)
     right_out(1, roots_1)
     lengths_turn(0)
-    lengths_turn(1)
     swap[2].wait_recv()
     each(NX, lambda d: gates_back(d).wait_recv())
     loads[6].wait()
@@ -428,15 +429,17 @@
     upper = ga[:, 2 * H : 4 * H]
     hid[...] = (gate * jax.nn.sigmoid(gate) * upper).astype(BF16)
 
-    out = jnp.dot(hid[...], d16[:, 0:W], preferred_element_type=F32)
-    for p in range(NY):
-        asrc[p] = out[ZT * p : ZT * p + ZT].astype(BF16)
-    each(NY, lambda d: sum_a1(d).start())
+    lengths_turn(1)
     turned = jnp.dot(perm[...], hid[...], preferred_element_type=F32).astype(BF16)
-    out = jnp.dot(turned, d16[:, W:D], preferred_element_type=F32)
-    for p in range(NZ):
-        bsrc[p] = out[YT * p : YT * p + YT].astype(BF16)
-    each(NZ, lambda d: sum_b1(d).start())
+    for h in range(2):
+        out = jnp.dot(hid[...], d16[:, h * Q : h * Q + Q], preferred_element_type=F32)
+        for p in range(NY):
+            asrc[p, h] = out[ZT * p : ZT * p + ZT].astype(BF16)
+        each(NY, lambda d: sum_a1(d, h).start())
+        out = jnp.dot(turned, d16[:, W + h * Q : W + h * Q + Q], preferred_element_type=F32)
+        for p in range(NZ):
+            bsrc[p, h] = out[YT * p : YT * p + YT].astype(BF16)
+        each(NZ, lambda d: sum_b1(d, h).start())
     adst[y] = asrc[y]
     bdst[z] = bsrc[z]
 
@@ -461,26 +464,29 @@
     each(NX, lambda d: gates_out(d).wait_send())
     each(NX, lambda d: gates_back(d).wait_send())
 
-    each(NY, lambda d: sum_a1(d).wait_recv())
-    total = adst[0].astype(F32)
-    for p in range(1, NY):
-        total = total + adst[p].astype(F32)
-    acc[...] = total
-    for p in range(NZ):
-        aq[p] = acc[T * p : T * p + T, :].astype(BF16)
-    each(NZ, lambda d: sum_a2(d).start())
-    ar[z] = aq[z]
-    each(NZ, lambda d: sum_b1(d).wait_recv())
-    total = bdst[0].astype(F32)
-    for p in range(1, NZ):
-        total = total + bdst[p].astype(F32)
-    acc[...] = total
+    for h in range(2):
+        each(NY, lambda d: sum_a1(d, h).wait_recv())
+        total = adst[0, h].astype(F32)
+        for p in range(1, NY):
+            total = total + adst[p, h].astype(F32)
+        acc[:, h * Q : h * Q + Q] = total
+        if h == 1:
+            for p in range(NZ):
+                aq[p] = acc[T * p : T * p + T, :].astype(BF16)
+            each(NZ, lambda d: sum_a2(d).start())
+            ar[z] = aq[z]
+        each(NZ, lambda d: sum_b1(d, h).wait_recv())
+        total = bdst[0, h].astype(F32)
+        for p in range(1, NZ):
+            total = total + bdst[p, h].astype(F32)
+        acb[:, h * Q : h * Q + Q] = total
     for p in range(NY):
-        bq[p] = acc[T * p : T * p + T, :].astype(BF16)
+        bq[p] = acb[T * p : T * p + T, :].astype(BF16)
     each(NY, lambda d: sum_b2(d).start())
     br[y] = bq[y]
-    each(NY, lambda d: sum_a1(d).wait_send())
-    each(NZ, lambda d: sum_b1(d).wait_send())
+    for h in range(2):
+        each(NY, lambda d: sum_a1(d, h).wait_send())
+        each(NZ, lambda d: sum_b1(d, h).wait_send())
     each(NZ, lambda d: sum_a2(d).wait_recv())
     total = ar[0].astype(F32)
     for p in range(1, NZ):
@@ -519,6 +525,7 @@
         NT = NY * ZT
         XT = NT // NX
         W = D // 2
+        Q = W // 2
         YT = NY * T
         dims = (NX, NY, NZ, H, D, T, D * NX, H * rows)
         V = pltpu.VMEM
@@ -550,7 +557,8 @@
                 V((NY, ZT, W), BF16), V((NZ, YT, W), BF16), V((NT, W), F32), V((NT, D), BF16), V((NT, NT), BF16),
                 *(ref for g in range(2) for ref in group((2, 4)[g], (1, 2)[g])),
                 V((NT, 4 * H), F32), V((NX, XT, 4 * H), F32), V((NT, 4 * H), F32), V((NT, 2 * H), BF16),
-                V((NY, ZT, W), BF16), V((NY, ZT, W), BF16), V((NZ, YT, W), BF16), V((NZ, YT, W), BF16), V((ZT, W), F32),
+                V((NY, 2, ZT, Q), BF16), V((NY, 2, ZT, Q), BF16), V((NZ, 2, YT, Q), BF16), V((NZ, 2, YT, Q), BF16),
+                V((ZT, W), F32), V((YT, W), F32),
                 V((NZ, T, W), BF16), V((NZ, T, W), BF16), V((NY, T, W), BF16), V((NY, T, W), BF16),
                 dma((3,)), dma((4,)),
                 dma((2, 2, NP)), dma((2, 2, NP)), dma((2, 2, NY)), dma((2, 2, NY)), dma((2, 2, NP)), dma((2, 2, NP)),
@@ -558,7 +566,7 @@
                 dma((2, NP)), dma((2, NP)), dma((2, NY)), dma((2, NY)), dma((3,)), dma((3,)),
                 dma((NZ,)), dma((NZ,)), dma((NY,)), dma((NY,)), dma((NY,)), dma((NY,)), dma((NZ,)), dma((NZ,)),
                 dma((NX,)), dma((NX,)), dma((NX,)), dma((NX,)),
-                dma((NY,)), dma((NY,)), dma((NZ,)), dma((NZ,)), dma((NZ,)), dma((NZ,)), dma((NY,)), dma((NY,)),
+                dma((2, NY)), dma((2, NY)), dma((2, NZ)), dma((2, NZ)), dma((NZ,)), dma((NZ,)), dma((NY,)), dma((NY,)),
             ],
             compiler_params=pltpu.CompilerParams(
                 collective_id=0, has_side_effects=True, vmem_limit_bytes=60 * 1024 * 1024

time: 84.7 us -> 83.4 us (0.985)
  Pallas kernels: 83.9 us -> 81.9 us
    pallas_call x1, Pallas kernels: 83.3 us -> 81.3 us  [per_device(): pl.pallas_call(functools.partial(kernel, dims), out_shape=(V((T, D), BF16...]
where the time goes in v4:
time: 83.4 us; the launch traced here: 82.6 us
  Pallas kernels  81.9 us (98%)
    pallas_call x1, Pallas kernels, per_device(): pl.pallas_call(functools.partial(kernel, dims), out_shape=(V((T, D), BF16...  81.3 us

profile of v4, /device:TPU:6, one launch (start us, length us, event | category | flops | bytes accessed | tf_op | source)
XLA Modules:
  0.0 82.6 jit_solution(664221587349672943)
XLA Ops:
  0.6 81.3 %shard_map.85 = (bf16[3,2048]{1,0:T(4,128)(2,1)S(1)}, f32[3,192]{1,0:T(4,128)S(1)}, f32[3,2048]{1,0:T(4,128)S(1)}) custom-call(bf16[3,2048]{1,0:T(4,128)(2,1)} %tok_h.1, f32[192,2048]{1,0:T(8,128)} %wg_h.1, f32[192,2048]{1,0:T(8,128)} %wu_h.1, f32[192,2048]{1,0:T(8,128)} %wd_h.1, f32[3,192]{1,0:T(4,128)} %ui_h.1, f32[3]{0:T(128)} %gam_h.1), custom_call_target="tpu_custom_call" | custom-call | tf_op jit(solution)/shard_map/pallas_call | solution.py:544
  81.9 0.7 shard_map.86

commit v5 on v4

--- a/solution.py
+++ b/solution.py
@@ -21,10 +21,10 @@
     gam, w, w16, d16, ui, ta, tb, tzf, xa, xb, xf, x16, perm,
     part_0, r1b_0, r1s_0, r2b_0, r2s_0, bv_0, bn_0, pk_0, cb_0, s3_0, r3b_0, s4_0, r4b_0,
     part_1, r1b_1, r1s_1, r2b_1, r2s_1, bv_1, bn_1, pk_1, cb_1, s3_1, r3b_1, s4_1, r4b_1,
-    gp, xr, ga, hid, asrc, adst, bsrc, bdst, acc, acb, aq, ar, bq, br,
+    gp, xr, ga, hid, asrc, adst, apre, bsrc, bdst, bpre, acc, acb, aq, ar, bq, br,
     wsem, lsem, p1s, p1r, p2s, p2r, p3s, p3r, cs, cr,
     e1s, e1r, e2s, e2r, ks, kr, ta1s, ta1r, tb1s, tb1r, ta2s, ta2r, tb2s, tb2r,
-    gs, gr, hs, hr, as1, ar1, bs1, br1, as2, ar2, bs2, br2,
+    gs, gr, hs, hr, as1, ar1, ap1, aq1, bs1, br1, bp1, bq1, as2, ar2, bs2, br2,
 ):
     NX, NY, NZ, H, D, T, DT, FT = dims
     FIRST, N, ROWS = (0, 1), (1, 2), (2, 4)
@@ -318,10 +318,43 @@
         return remote(mine, mine, hs.at[d], hr.at[d], row, along_x(d))
 
     def sum_a1(d, h):
-        return remote(asrc.at[along_y(d)[0], h], adst.at[y, h], as1.at[h, d], ar1.at[h, d], along_y(d)[1], x)
+        return remote(asrc.at[along_y(d)[0], h], adst.at[d, h], as1.at[h, d], ar1.at[h, d], along_y(d)[1], x)
 
     def sum_b1(d, h):
-        return remote(bsrc.at[along_z(d)[0], h], bdst.at[z, h], bs1.at[h, d], br1.at[h, d], along_z(d)[1], x)
+        return remote(bsrc.at[along_z(d)[0], h], bdst.at[d, h], bs1.at[h, d], br1.at[h, d], along_z(d)[1], x)
+
+    def pre_a1(h):
+        d = (1, NY - 1)[h]
+        return remote(asrc.at[along_y(NY // 2)[0], h], apre.at[h], ap1.at[h], aq1.at[h], along_y(d)[1], x)
+
+    def pre_b1(h):
+        d = (1, NZ - 1)[h]
+        return remote(bsrc.at[along_z(NZ // 2)[0], h], bpre.at[h], bp1.at[h], bq1.at[h], along_z(d)[1], x)
+
+    def joined(n, h):
+        return (n // 2 - 1, n // 2 + 1)[h]
+
+    def direct(n, h):
+        near = [d for d in range(1, n) if d not in (n // 2, joined(n, h))]
+        return sorted(near, key=lambda d: -min(d, n - d))
+
+    def early(n):
+        return [d for d in direct(n, 0) if d < n // 2 or d == n - 1]
+
+    def late(n):
+        return [d for d in direct(n, 0) if d not in early(n)]
+
+    def join_a1(h):
+        p = along_y(joined(NY, h))[0]
+        pre_a1(h).wait_recv()
+        asrc[p, h] = (asrc[p, h].astype(F32) + apre[h].astype(F32)).astype(BF16)
+        sum_a1(joined(NY, h), h).start()
+
+    def join_b1(h):
+        p = along_z(joined(NZ, h))[0]
+        pre_b1(h).wait_recv()
+        bsrc[p, h] = (bsrc[p, h].astype(F32) + bpre[h].astype(F32)).astype(BF16)
+        sum_b1(joined(NZ, h), h).start()
 
     def sum_a2(d):
         return remote(aq.at[along_z(d)[0]], ar.at[z], as2.at[d], ar2.at[d], along_z(d)[1], x)
@@ -435,16 +468,29 @@
         out = jnp.dot(hid[...], d16[:, h * Q : h * Q + Q], preferred_element_type=F32)
         for p in range(NY):
             asrc[p, h] = out[ZT * p : ZT * p + ZT].astype(BF16)
-        each(NY, lambda d: sum_a1(d, h).start())
+        pre_a1(h).start()
+        for d in (early(NY), direct(NY, 1))[h]:
+            sum_a1(d, h).start()
+        if h == 1:
+            for d in late(NY):
+                sum_a1(d, 0).start()
         out = jnp.dot(turned, d16[:, W + h * Q : W + h * Q + Q], preferred_element_type=F32)
         for p in range(NZ):
             bsrc[p, h] = out[YT * p : YT * p + YT].astype(BF16)
-        each(NZ, lambda d: sum_b1(d, h).start())
-    adst[y] = asrc[y]
-    bdst[z] = bsrc[z]
+        pre_b1(h).start()
+        for d in (early(NZ), direct(NZ, 1))[h]:
+            sum_b1(d, h).start()
+        if h == 1:
+            for d in late(NZ):
+                sum_b1(d, 0).start()
+    adst[0] = asrc[y]
+    bdst[0] = bsrc[z]
+    left_out(0, fore_0, lengths_0)
+    for h in range(2):
+        join_a1(h)
+        join_b1(h)
 
     lengths_1, scales_1 = lengths_finish(1)
-    left_out(0, fore_0, lengths_0)
     left_out(1, fore_1, lengths_1)
 
     for g in range(2):
@@ -465,28 +511,34 @@
     each(NX, lambda d: gates_back(d).wait_send())
 
     for h in range(2):
-        each(NY, lambda d: sum_a1(d, h).wait_recv())
         total = adst[0, h].astype(F32)
-        for p in range(1, NY):
-            total = total + adst[p, h].astype(F32)
+        for d in direct(NY, h) + [joined(NY, h)]:
+            sum_a1(d, h).wait_recv()
+        for d in direct(NY, h) + [joined(NY, h)]:
+            total = total + adst[d, h].astype(F32)
         acc[:, h * Q : h * Q + Q] = total
         if h == 1:
             for p in range(NZ):
                 aq[p] = acc[T * p : T * p + T, :].astype(BF16)
             each(NZ, lambda d: sum_a2(d).start())
             ar[z] = aq[z]
-        each(NZ, lambda d: sum_b1(d, h).wait_recv())
         total = bdst[0, h].astype(F32)
-        for p in range(1, NZ):
-            total = total + bdst[p, h].astype(F32)
+        for d in direct(NZ, h) + [joined(NZ, h)]:
+            sum_b1(d, h).wait_recv()
+        for d in direct(NZ, h) + [joined(NZ, h)]:
+            total = total + bdst[d, h].astype(F32)
         acb[:, h * Q : h * Q + Q] = total
     for p in range(NY):
         bq[p] = acb[T * p : T * p + T, :].astype(BF16)
     each(NY, lambda d: sum_b2(d).start())
     br[y] = bq[y]
     for h in range(2):
-        each(NY, lambda d: sum_a1(d, h).wait_send())
-        each(NZ, lambda d: sum_b1(d, h).wait_send())
+        pre_a1(h).wait_send()
+        pre_b1(h).wait_send()
+        for d in direct(NY, h) + [joined(NY, h)]:
+            sum_a1(d, h).wait_send()
+        for d in direct(NZ, h) + [joined(NZ, h)]:
+            sum_b1(d, h).wait_send()
     each(NZ, lambda d: sum_a2(d).wait_recv())
     total = ar[0].astype(F32)
     for p in range(1, NZ):
@@ -557,7 +609,8 @@
                 V((NY, ZT, W), BF16), V((NZ, YT, W), BF16), V((NT, W), F32), V((NT, D), BF16), V((NT, NT), BF16),
                 *(ref for g in range(2) for ref in group((2, 4)[g], (1, 2)[g])),
                 V((NT, 4 * H), F32), V((NX, XT, 4 * H), F32), V((NT, 4 * H), F32), V((NT, 2 * H), BF16),
-                V((NY, 2, ZT, Q), BF16), V((NY, 2, ZT, Q), BF16), V((NZ, 2, YT, Q), BF16), V((NZ, 2, YT, Q), BF16),
+                V((NY, 2, ZT, Q), BF16), V((NY, 2, ZT, Q), BF16), V((2, ZT, Q), BF16),
+                V((NZ, 2, YT, Q), BF16), V((NZ, 2, YT, Q), BF16), V((2, YT, Q), BF16),
                 V((ZT, W), F32), V((YT, W), F32),
                 V((NZ, T, W), BF16), V((NZ, T, W), BF16), V((NY, T, W), BF16), V((NY, T, W), BF16),
                 dma((3,)), dma((4,)),
@@ -566,7 +619,8 @@
                 dma((2, NP)), dma((2, NP)), dma((2, NY)), dma((2, NY)), dma((3,)), dma((3,)),
                 dma((NZ,)), dma((NZ,)), dma((NY,)), dma((NY,)), dma((NY,)), dma((NY,)), dma((NZ,)), dma((NZ,)),
                 dma((NX,)), dma((NX,)), dma((NX,)), dma((NX,)),
-                dma((2, NY)), dma((2, NY)), dma((2, NZ)), dma((2, NZ)), dma((NZ,)), dma((NZ,)), dma((NY,)), dma((NY,)),
+                dma((2, NY)), dma((2, NY)), dma((2,)), dma((2,)), dma((2, NZ)), dma((2, NZ)), dma((2,)), dma((2,)),
+                dma((NZ,)), dma((NZ,)), dma((NY,)), dma((NY,)),
             ],
             compiler_params=pltpu.CompilerParams(
                 collective_id=0, has_side_effects=True, vmem_limit_bytes=60 * 1024 * 1024

time: 83.4 us -> 83.1 us (level)
  no operation moved by 1% of the time
where the time goes in v5:
time: 83.1 us; the launch traced here: 83 us
  Pallas kernels  82.4 us (99%)
    pallas_call x1, Pallas kernels, per_device(): pl.pallas_call(functools.partial(kernel, dims), out_shape=(V((T, D), BF16...  81.7 us

profile of v5, /device:TPU:6, one launch (start us, length us, event | category | flops | bytes accessed | tf_op | source)
XLA Modules:
  0.0 83.0 jit_solution(388151163100137554)
XLA Ops:
  0.6 81.7 %shard_map.85 = (bf16[3,2048]{1,0:T(4,128)(2,1)S(1)}, f32[3,192]{1,0:T(4,128)S(1)}, f32[3,2048]{1,0:T(4,128)S(1)}) custom-call(bf16[3,2048]{1,0:T(4,128)(2,1)} %tok_h.1, f32[192,2048]{1,0:T(8,128)} %wg_h.1, f32[192,2048]{1,0:T(8,128)} %wu_h.1, f32[192,2048]{1,0:T(8,128)} %wd_h.1, f32[3,192]{1,0:T(4,128)} %ui_h.1, f32[3]{0:T(128)} %gam_h.1), custom_call_target="tpu_custom_call" | custom-call | tf_op jit(solution)/shard_map/pallas_call | solution.py:596
  82.4 0.7 shard_map.86

commit v6 on v5

--- a/solution.py
+++ b/solution.py
@@ -381,7 +381,6 @@
     for p in range(NZ):
         tzf[T * p : T * p + T, :] = ta[p].astype(F32)
     xa[y] = tzf[...].astype(BF16)
-    each(NY, lambda d: tok_a2(d).start())
     loads[5].wait()
     each(NY, lambda d: tok_b1(d).wait_recv())
     for p in range(NY):
@@ -399,6 +398,7 @@
     perm[...] = jnp.where(hi == wanted, 1.0, 0.0).astype(BF16)
     start3(0, 0)
     start3(1, 0)
+    each(NY, lambda d: tok_a2(d).start())
     each(NZ, lambda d: tok_b2(d).start())
     finish3(0, 0)
     col_start(0, 0, fore_packed(0, bv[0].at[0]))

time: 83.1 us -> 81.5 us (0.981)
  Pallas kernels: 82.4 us -> 80.2 us
    pallas_call x1, Pallas kernels: 81.7 us -> 79.5 us  [per_device(): pl.pallas_call(functools.partial(kernel, dims), out_shape=(V((T, D), BF16...]
where the time goes in v6:
time: 81.5 us; the launch traced here: 80.8 us
  Pallas kernels  80.2 us (98%)
    pallas_call x1, Pallas kernels, per_device(): pl.pallas_call(functools.partial(kernel, dims), out_shape=(V((T, D), BF16...  79.5 us

profile of v6, /device:TPU:6, one launch (start us, length us, event | category | flops | bytes accessed | tf_op | source)
XLA Modules:
  0.0 80.8 jit_solution(13096316387058865090)
XLA Ops:
  0.6 79.5 %shard_map.85 = (bf16[3,2048]{1,0:T(4,128)(2,1)S(1)}, f32[3,192]{1,0:T(4,128)S(1)}, f32[3,2048]{1,0:T(4,128)S(1)}) custom-call(bf16[3,2048]{1,0:T(4,128)(2,1)} %tok_h.1, f32[192,2048]{1,0:T(8,128)} %wg_h.1, f32[192,2048]{1,0:T(8,128)} %wu_h.1, f32[192,2048]{1,0:T(8,128)} %wd_h.1, f32[3,192]{1,0:T(4,128)} %ui_h.1, f32[3]{0:T(128)} %gam_h.1), custom_call_target="tpu_custom_call" | custom-call | tf_op jit(solution)/shard_map/pallas_call | solution.py:596
  80.2 0.7 shard_map.86
